TPU v7x, 256 devices: a whole 4x4x8 slice. The times are simulated.
256 devices in a mesh: seg: 4 (over y), ep: 64 (over z, x, core).
Axes of the slice: x: 4, y: 4, z: 8, core: 2. Of those that a mesh axis runs over, the one named last changes fastest.
Arguments:
- frames_in: bfloat16 [32768, 2048], P(('seg', 'ep')), may hold values from -36 to 36
- expert_ids: int32 [32768, 6], P(('seg', 'ep')), may hold values from 0 to 63, all different within a row
- gate_values: float32 [32768, 6], P(('seg', 'ep')), may hold values from 0.02 to 0.3
- gate_weight: bfloat16 [64, 2048, 768], P('ep'), may hold values from -0.125 to 0.125
- up_weight: bfloat16 [64, 2048, 768], P('ep'), may hold values from -0.125 to 0.125
- down_weight: bfloat16 [64, 768, 2048], P('ep'), may hold values from -0.21875 to 0.21875
- norm_gain: float32 [2048], replicated, may hold values from 0.5 to 1.5
- pose_weight: bfloat16 [2048, 256], replicated, may hold values from -0.125 to 0.125
- target_pose: float32 [32768, 256], P(('seg', 'ep')), may hold values from -6 to 6
- foot_contact: int32 [32768, 4], P(('seg', 'ep')), may hold values 0 or 1
Outputs:
- grad_input: bfloat16 [32768, 2048], P(('seg', 'ep'))
- grad_gates: float32 [32768, 6], P(('seg', 'ep'))
- loss_value: float32 [], replicated
Inputs may be any that keep to these rules, and one draw needn't show every extreme that they name: `expert_ids`: each row names 6 different experts.
All inputs are finite; a program needn't handle non-finite values. No bound on the sum of `foot_contact` on one device may be relied on, other than what follows from the above.
Results may differ from a plain program's by a relative error of at most 0.011.
Values may be sent and summed in bfloat16 or wider, within the bound.
A program may use at most 128 MiB of HBM per device.

v0:
```python
import jax
import jax.numpy as jnp
from jax import lax
from jax.sharding import PartitionSpec as P

epsilon = 1e-06
foot_weight = 2.0


def from_behind(block, axis, distance):
    devices = range(lax.axis_size(axis))
    route = [(i - distance, i) for i in devices if i - distance in devices]
    return lax.ppermute(block, axis, route)


def silu_parts(pre_act):
    gate_sigmoid = jax.nn.sigmoid(pre_act)
    return (pre_act * gate_sigmoid, gate_sigmoid * (1.0 + pre_act * (1.0 - gate_sigmoid)))


def foot_term(horizon, contact_rep, velocity):
    return foot_weight * horizon[:, None] * contact_rep * velocity


def slot_tables(expert_ids, experts, capacity):
    pair_count = expert_ids.shape[0] * expert_ids.shape[1]
    flat_ids = expert_ids.reshape(-1)
    onehot = (flat_ids[:, None] == jnp.arange(experts, dtype=jnp.int32)[None, :]).astype(jnp.int32)
    earlier_hits = jnp.cumsum(onehot, axis=0) - onehot
    slot_rank = jnp.sum(earlier_hits * onehot, axis=1)
    kept_mask = slot_rank < capacity
    spare_slot = experts * capacity
    position = jnp.where(kept_mask, flat_ids * capacity + slot_rank, spare_slot)
    pair_of_slot = (
        jnp.full((spare_slot + 1,), pair_count, jnp.int32)
        .at[position]
        .set(jnp.arange(pair_count, dtype=jnp.int32))[:spare_slot]
    )
    return (position, pair_of_slot)


def per_device(
    frames_in,
    expert_ids,
    gate_values,
    gate_weight,
    up_weight,
    down_weight,
    norm_gain,
    pose_weight,
    target_pose,
    foot_contact,
):
    tok_rows, model_width = frames_in.shape
    top_count = expert_ids.shape[1]
    local_experts = gate_weight.shape[0]
    ep_count = lax.axis_size("ep")
    experts = local_experts * ep_count
    capacity = tok_rows * top_count // experts
    position, pair_of_slot = slot_tables(expert_ids, experts, capacity)
    token_of_slot = pair_of_slot // top_count
    zero_row = jnp.zeros((1, model_width), jnp.bfloat16)
    padded_in = jnp.concatenate([frames_in, zero_row], 0)
    send_rows = padded_in[token_of_slot].reshape(experts, capacity, model_width)
    received = lax.all_to_all(send_rows, "ep", split_axis=0, concat_axis=0, tiled=True)
    slot_count = received.shape[1]
    grouped = received.reshape(ep_count, local_experts, slot_count, model_width)
    gate_pre = jnp.einsum(
        "sexd,edf->sexf", grouped, gate_weight, preferred_element_type=jnp.float32
    )
    up_pre = jnp.einsum("sexd,edf->sexf", grouped, up_weight, preferred_element_type=jnp.float32)
    activated = silu_parts(gate_pre)[0]
    hidden = (activated * up_pre).astype(jnp.bfloat16)
    produced = jnp.einsum(
        "sexf,efd->sexd", hidden, down_weight, preferred_element_type=jnp.float32
    ).astype(jnp.bfloat16)
    produced = produced.reshape(experts, slot_count, model_width)
    returned = lax.all_to_all(produced, "ep", split_axis=0, concat_axis=0, tiled=True)
    hidden_width = gate_pre.shape[-1]
    returned, produced_local, gate_keep, up_keep = (
        returned,
        produced,
        gate_pre.reshape(experts, slot_count, hidden_width),
        up_pre.reshape(experts, slot_count, hidden_width),
    )
    back_flat = jnp.concatenate([returned.reshape(experts * capacity, model_width), zero_row], 0)
    picked = back_flat[position].reshape(tok_rows, top_count, model_width)
    mixed_rows = jnp.sum(gate_values[:, :, None] * picked, axis=1)
    state_rows = frames_in.astype(jnp.float32) + mixed_rows
    inverse_rms = lax.rsqrt(jnp.mean(state_rows * state_rows, axis=1, keepdims=True) + epsilon)
    unit_rows = state_rows * inverse_rms
    normed = (unit_rows * norm_gain).astype(jnp.bfloat16)
    pose_out = jnp.dot(normed, pose_weight, preferred_element_type=jnp.float32)
    pose_cols = pose_out.shape[1]
    device = lax.axis_index("seg") * ep_count + lax.axis_index("ep")
    frames_all = lax.axis_size("seg") * ep_count * tok_rows
    frame_index = device * tok_rows + jnp.arange(tok_rows, dtype=jnp.int32)
    horizon = 0.5 + frame_index.astype(jnp.float32) / (frames_all - 1)
    feet_count = foot_contact.shape[1]
    foot_cols = 3 * feet_count
    foot_pos = pose_out[:, :foot_cols]
    contact_float = foot_contact.astype(jnp.float32)
    contact_rep = jnp.repeat(contact_float, 3, axis=1)
    before = from_behind(foot_pos[tok_rows - 1 :], ("seg", "ep"), 1)
    earlier = jnp.concatenate([before, foot_pos[:-1]], 0)
    velocity = jnp.where((frame_index > 0)[:, None], foot_pos - earlier, 0.0)
    foot_pull = foot_term(horizon, contact_rep, velocity)
    next_pull = from_behind(foot_pull[:1], ("seg", "ep"), -1)
    pose_error = pose_out - target_pose
    local_sum = 0.5 * jnp.sum(horizon[:, None] * pose_error * pose_error) + 0.5 * jnp.sum(
        foot_pull * velocity
    )
    summed = lax.psum(local_sum, ("seg", "ep"))
    loss_value = summed / (frames_all * pose_cols)
    later_pull = jnp.concatenate([foot_pull[1:], next_pull], 0)
    grad_pose = horizon[:, None] * pose_error
    grad_pose = jnp.concatenate(
        [grad_pose[:, :foot_cols] + (foot_pull - later_pull), grad_pose[:, foot_cols:]], 1
    )
    grad_normed = jnp.einsum(
        "tp,dp->td", grad_pose.astype(jnp.bfloat16), pose_weight, preferred_element_type=jnp.float32
    )
    scaled = grad_normed * norm_gain
    grad_state = inverse_rms * (
        scaled - unit_rows * jnp.mean(scaled * unit_rows, axis=1, keepdims=True)
    )
    moe_grad = grad_state.astype(jnp.bfloat16)
    pair_grad = (gate_values[:, :, None] * moe_grad[:, None, :]).astype(jnp.bfloat16)
    pair_flat = jnp.concatenate([pair_grad.reshape(tok_rows * top_count, model_width), zero_row], 0)
    grad_send = pair_flat[pair_of_slot].reshape(experts, capacity, model_width)
    arrived = lax.all_to_all(grad_send, "ep", split_axis=0, concat_axis=0, tiled=True)
    slot_count = arrived.shape[1]
    hidden_width = gate_keep.shape[-1]
    grouped = arrived.reshape(ep_count, local_experts, slot_count, model_width)
    gate_pre = gate_keep.reshape(ep_count, local_experts, slot_count, hidden_width)
    up_pre = up_keep.reshape(ep_count, local_experts, slot_count, hidden_width)
    grad_hidden = jnp.einsum(
        "sexd,efd->sexf", grouped, down_weight, preferred_element_type=jnp.float32
    )
    activated, silu_slope = silu_parts(gate_pre)
    grad_gate_pre = (grad_hidden * up_pre * silu_slope).astype(jnp.bfloat16)
    grad_up_pre = (grad_hidden * activated).astype(jnp.bfloat16)
    grad_rows = jnp.einsum(
        "sexf,edf->sexd", grad_gate_pre, gate_weight, preferred_element_type=jnp.float32
    )
    grad_rows = grad_rows + jnp.einsum(
        "sexf,edf->sexd", grad_up_pre, up_weight, preferred_element_type=jnp.float32
    )
    grad_rows = grad_rows.astype(jnp.bfloat16).reshape(experts, slot_count, model_width)
    grad_back = lax.all_to_all(grad_rows, "ep", split_axis=0, concat_axis=0, tiled=True)
    grad_gates = jnp.einsum("tkd,td->tk", picked, moe_grad, preferred_element_type=jnp.float32)
    grad_flat = jnp.concatenate([grad_back.reshape(experts * capacity, model_width), zero_row], 0)
    grad_picked = grad_flat[position].reshape(tok_rows, top_count, model_width)
    grad_input = (grad_state + jnp.sum(grad_picked.astype(jnp.float32), axis=1)).astype(
        jnp.bfloat16
    )
    return (grad_input, grad_gates, loss_value)


def solution(mesh):
    in_specs = (
        P(("seg", "ep"), None),
        P(("seg", "ep"), None),
        P(("seg", "ep"), None),
        P("ep", None, None),
        P("ep", None, None),
        P("ep", None, None),
        P(),
        P(),
        P(("seg", "ep"), None),
        P(("seg", "ep"), None),
    )
    out_specs = (P(("seg", "ep"), None), P(("seg", "ep"), None), P())
    return jax.shard_map(
        per_device, mesh=mesh, in_specs=in_specs, out_specs=out_specs, check_vma=False
    )
```

profile of v0, /device:TPU:1, one launch (start us, length us, event | category | flops | bytes accessed | tf_op | source)
XLA Modules:
  0.0 645.0 jit_solution(18310391385178528814)
XLA Ops:
  0.6 0.8 broadcast_multiply_fusion.1
  1.5 0.9 copy.45
  2.9 1.8 reduce-window.6
  5.2 3.4 scatter_custom_fusion
  8.7 1.9 concatenate.22
  10.5 8.2 %gather_fusion = bf16[768,2048]{1,0:T(8,128)(2,1)} fusion(bf16[129,2048]{1,0:T(8,128)(2,1)} %concatenate.22, s32[1024]{0:T(1024)S(1)} %get-tuple-element.15), kind=kCustom, calls=%fused_computation | custom fusion | bytes 6294528 | tf_op jit(solution)/shard_map/gather | solution.py:64
  18.8 6.1 reshape.153
  24.9 108.0 %all_to_all.20 = bf16[64,12,2048]{2,1,0:T(8,128)(2,1)S(1)} all-to-all(bf16[64,12,2048]{2,1,0:T(8,128)(2,1)} %reshape.153), channel_id=1, replica_groups=mesh['seg'=4,'ep'=64] {'ep'}, dimensions={0} | all-to-all | bytes 6291456 | tf_op jit(solution)/shard_map/all_to_all | solution.py:65
  132.9 6.1 fusion.8
  139.0 6.1 fusion.4
  145.1 3.3 convolution_convert_fusion
  148.5 3.7 copy.51
  152.2 7.4 %all-to-all-start.1 = ((bf16[64,12,2048]{2,1,0:T(8,128)(2,1)}), bf16[64,12,2048]{2,1,0:T(8,128)(2,1)}, u32[]{:S(2)}, u32[]{:S(2)}) async-start(bf16[64,12,2048]{2,1,0:T(8,128)(2,1)} %copy.51), calls=%async_computation.1 | async-start | bytes 8388608 | tf_op jit(solution)/shard_map/all_to_all | solution.py:78
  160.1 94.1 %all-to-all-done.1 = bf16[64,12,2048]{2,1,0:T(8,128)(2,1)} async-done(((bf16[64,12,2048]{2,1,0:T(8,128)(2,1)}), bf16[64,12,2048]{2,1,0:T(8,128)(2,1)}, u32[]{:S(2)}, u32[]{:S(2)}) %all-to-all-start.1) | async-done | bytes 3145760 | tf_op jit(solution)/shard_map/all_to_all | solution.py:78
  254.1 6.2 reshape.158
  260.3 4.0 concatenate.23
  264.3 9.4 %gather_fusion.1 = bf16[768,2048]{1,0:T(8,128)(2,1)} fusion(bf16[769,2048]{1,0:T(8,128)(2,1)} %concatenate.23, s32[1024]{0:T(1024)S(1)} %pad_clamp_fusion.1), kind=kCustom, calls=%fused_computation.1 | custom fusion | bytes 6294528 | tf_op jit(solution)/shard_map/gather | solution.py:87
  273.7 6.3 reshape.159
  280.0 5.7 multiply_reduce_fusion
  285.9 1.0 multiply_reduce_fusion.3
  286.9 5.2 collective-permute-start
  292.2 0.6 collective-permute-done
  292.8 0.7 multiply_reduce_fusion.4
  293.5 1.9 collective-permute-start.1
  295.4 3.4 collective-permute-done.1
  299.5 1.2 convert_bitcast_fusion
  300.7 1.0 copy-done.2
  301.7 4.3 mul.184
  306.0 8.3 %mul.185 = f32[768,2048]{1,0:T(8,128)} reshape(f32[128,6,2048]{2,1,0:T(8,128)} %mul.184) | data formatting | bytes 12582912 | tf_op jit(solution)/shard_map/mul | solution.py:128
  314.2 3.2 multiply_convert_fusion
  317.4 2.0 concatenate.27
  319.4 9.4 %gather_fusion.2 = bf16[768,2048]{1,0:T(8,128)(2,1)} fusion(bf16[769,2048]{1,0:T(8,128)(2,1)} %concatenate.27, s32[1024]{0:T(1024)S(1)} %get-tuple-element.14), kind=kCustom, calls=%fused_computation.2 | custom fusion | bytes 6294528 | tf_op jit(solution)/shard_map/gather | solution.py:130
  328.9 6.1 reshape.161
  334.9 105.9 %all_to_all.21 = bf16[64,12,2048]{2,1,0:T(8,128)(2,1)S(1)} all-to-all(bf16[64,12,2048]{2,1,0:T(8,128)(2,1)} %reshape.161), channel_id=1, replica_groups=mesh['seg'=4,'ep'=64] {'ep'}, dimensions={0} | all-to-all | bytes 6291456 | tf_op jit(solution)/shard_map/all_to_all | solution.py:131
  440.8 6.1 fusion
  447.0 3.0 fusion.6
  450.0 2.9 add_convert_fusion
  452.9 3.7 copy.55
  456.7 7.3 %all-to-all-start.3 = ((bf16[64,12,2048]{2,1,0:T(8,128)(2,1)}), bf16[64,12,2048]{2,1,0:T(8,128)(2,1)}, u32[]{:S(2)}, u32[]{:S(2)}) async-start(bf16[64,12,2048]{2,1,0:T(8,128)(2,1)} %copy.55), calls=%async_computation.3 | async-start | bytes 8388608 | tf_op jit(solution)/shard_map/all_to_all | solution.py:150
  465.3 136.1 %psum.7 = f32[]{:T(128)} all-reduce(f32[]{:T(128)S(6)} %add.129), channel_id=1, replica_groups=mesh['seg'=4,'ep'=64] {'seg','ep'}, use_global_device_ids=true, to_apply=%region_10.11 | all-reduce | flops 1 | bytes 8 | tf_op jit(solution)/shard_map/psum | solution.py:113
  602.1 5.2 fusion.28
  607.3 0.7 copy.57
  608.0 6.2 reshape.164
  614.1 4.0 concatenate.28
  618.1 9.4 %gather_fusion.3 = bf16[768,2048]{1,0:T(8,128)(2,1)} fusion(bf16[769,2048]{1,0:T(8,128)(2,1)} %concatenate.28, s32[1024]{0:T(1024)S(1)} %pad_clamp_fusion.1), kind=kCustom, calls=%fused_computation.3 | custom fusion | bytes 6294528 | tf_op jit(solution)/shard_map/gather | solution.py:153
  627.5 6.6 %reshape.165 = f32[128,6,2048]{2,1,0:T(8,128)} reshape(bf16[768,2048]{1,0:T(8,128)(2,1)} %gather_fusion.3) | data formatting | bytes 9437184 | tf_op jit(solution)/shard_map/convert_element_type | solution.py:154
  634.0 7.1 %reduce_sum.70 = f32[128,2048]{1,0:T(8,128)} reduce(f32[128,6,2048]{2,1,0:T(8,128)} %reshape.165, f32[]{:T(128)} %constant.19.clone.1), dimensions={1}, to_apply=%region_7.8 | reduce | flops 1310720 | bytes 7340036 | tf_op jit(solution)/shard_map/reduce_sum | solution.py:154
  641.1 2.5 add_convert_fusion.1
  (65 shorter events, 2.5 us)
Async XLA Ops:
  0.6 144.5 %copy-start = (bf16[1,768,2048]{2,1,0:T(8,128)(2,1)S(1)}, bf16[1,768,2048]{2,1,0:T(8,128)(2,1)}, u32[]{:S(2)}) copy-start(bf16[1,768,2048]{2,1,0:T(8,128)(2,1)} %param.15) | copy-start | bytes 9437188
  24.9 108.0 %copy-start.8 = (bf16[1,2048,768]{2,1,0:T(8,128)(2,1)S(1)}, bf16[1,2048,768]{2,1,0:T(8,128)(2,1)}, u32[]{:S(2)}) copy-start(bf16[1,2048,768]{2,1,0:T(8,128)(2,1)} %param.13) | copy-start | bytes 9437188
  132.9 6.1 copy-start.10
  139.0 6.1 copy-start.12
  145.1 3.3 copy-start.14
  152.2 7.4 %copy-start.7 = (s32[128,4]{0,1:T(4,128)S(1)}, s32[128,4]{0,1:T(4,128)}, u32[]{:S(2)}) copy-start(s32[128,4]{0,1:T(4,128)} %param.19) | copy-start | bytes 6148
  152.2 7.5 %copy-start.6 = (f32[128,6]{0,1:T(8,128)S(1)}, f32[128,6]{0,1:T(8,128)}, u32[]{:S(2)}) copy-start(f32[128,6]{0,1:T(8,128)} %param.12) | copy-start | bytes 9220
  152.2 101.9 %all-to-all-start.1 = ((bf16[64,12,2048]{2,1,0:T(8,128)(2,1)}), bf16[64,12,2048]{2,1,0:T(8,128)(2,1)}, u32[]{:S(2)}, u32[]{:S(2)}) async-start(bf16[64,12,2048]{2,1,0:T(8,128)(2,1)} %copy.51), calls=%async_computation.1 | async-start | bytes 8388608 | tf_op jit(solution)/shard_map/all_to_all | solution.py:78
  279.9 5.7 copy-start.1
  279.9 5.9 copy-start.3
  279.9 6.0 copy-start.4
  279.9 6.0 copy-start.5
  286.9 5.9 collective-permute-start
  293.5 5.4 collective-permute-start.1
  300.7 1.0 copy-start.2
  440.8 6.1 copy-start.9
  440.8 6.2 copy-start.13
  440.8 6.2 copy-start.15
  447.0 3.0 copy-start.11
  456.7 151.3 %all-to-all-start.3 = ((bf16[64,12,2048]{2,1,0:T(8,128)(2,1)}), bf16[64,12,2048]{2,1,0:T(8,128)(2,1)}, u32[]{:S(2)}, u32[]{:S(2)}) async-start(bf16[64,12,2048]{2,1,0:T(8,128)(2,1)} %copy.55), calls=%async_computation.3 | async-start | bytes 8388608 | tf_op jit(solution)/shard_map/all_to_all | solution.py:150
where the time goes:
time: 651 us; the launch traced here: 645 us
  blocking collectives  350 us (54%)
  local copies, waits for them, and re-layouts  113 us (17%)
  waiting for transfers between devices  98.1 us (15%)
  matrix products  34.2 us (5%)
  other arithmetic  23.5 us (4%)
  starting transfers between devices  21.8 us (3%)
    psum x1, blocking collectives, per_device(): summed = lax.psum(local_sum, ('seg', 'ep'))  136 us
    all_to_all x1, blocking collectives, per_device(): lax.all_to_all(send_rows, 'ep', split_axis=0, concat_axis=0, tiled=True)  108 us
    all_to_all x1, blocking collectives, per_device(): lax.all_to_all(grad_send, 'ep', split_axis=0, concat_axis=0, tiled=True)  106 us
    all_to_all x1, waiting for transfers between devices, per_device(): lax.all_to_all(produced, 'ep', split_axis=0, concat_axis=0, tiled=True)  94.1 us
  transfers between devices with their start and end apart: 4, of which 3 were waited for; matrix products, arithmetic and copies ran while one was open for 1% of the time, Pallas kernels for 0%

commit v1 on v0

v1 whole, which is shorter than its diff:
```python
import functools

import jax
import jax.numpy as jnp
from jax import lax
from jax.experimental import pallas as pl
from jax.experimental.pallas import tpu as pltpu
from jax.sharding import PartitionSpec as P

MESH = pl.DeviceIdType.MESH
epsilon = 1e-06
foot_weight = 2.0

RING = 8
GROUP = 8
ROWS = 128
CAP = 12
TOP = 6
D = 2048
FFW = 768
CHUNK = 512
PAIR = 2 * CAP
BLOCK = GROUP * PAIR
F32 = jnp.float32
BF16 = jnp.bfloat16

PLACE = {0: 0, 1: 1, 7: 2, 2: 3, 6: 4, 3: 5, 5: 6, 4: 7}


def cols(c):
    return pl.ds(c * CHUNK, CHUNK)


class Place:
    def __init__(self):
        ep = lax.axis_index("ep")
        self.z = lax.div(ep, GROUP)
        self.g = lax.rem(ep, GROUP)

    def ring(self, distance):
        return {"ep": lax.rem(self.z + distance + RING, RING) * GROUP + self.g}

    def mate(self, offset):
        return lax.rem(self.g + offset, GROUP)

    def group(self, offset):
        return {"ep": self.z * GROUP + self.mate(offset)}

    def barrier(self):
        semaphore = pltpu.get_barrier_semaphore()
        for o in range(1, RING):
            pl.semaphore_signal(semaphore, inc=1, device_id=self.ring(o), device_id_type=MESH)
        for o in range(1, GROUP):
            pl.semaphore_signal(semaphore, inc=1, device_id=self.group(o), device_id_type=MESH)
        pl.semaphore_wait(semaphore, RING + GROUP - 2)


def remote(src, dst, send_sem, recv_sem, device):
    return pltpu.make_async_remote_copy(
        src_ref=src, dst_ref=dst, send_sem=send_sem, recv_sem=recv_sem,
        device_id=device, device_id_type=MESH,
    )


def slot_rows(ids_t, gates_t):
    experts = lax.broadcasted_iota(jnp.int32, (RING * GROUP, ROWS), 0)
    chosen = jnp.zeros((RING * GROUP, ROWS), F32)
    for k in range(TOP):
        chosen = chosen + jnp.where(ids_t[k : k + 1, :] == experts, 1.0, 0.0)
    before = lax.broadcasted_iota(jnp.int32, (ROWS, ROWS), 0) < lax.broadcasted_iota(
        jnp.int32, (ROWS, ROWS), 1
    )
    earlier = jnp.dot(
        chosen.astype(BF16), jnp.where(before, 1.0, 0.0).astype(BF16), preferred_element_type=F32
    )
    table = []
    for k in range(TOP):
        ids = ids_t[k : k + 1, :]
        rank = jnp.sum(jnp.where(ids == experts, earlier, 0.0), axis=0, keepdims=True)
        table.append(jnp.where(rank < CAP, ids.astype(F32) * CAP + rank, -1.0))
    table.append(jnp.full((2, ROWS), -1.0, F32))
    return jnp.concatenate(table + [gates_t], axis=0)


def row_slots(z, half):
    r = lax.broadcasted_iota(jnp.int32, (256, ROWS), 0)
    dest = jnp.zeros((256, ROWS), jnp.int32)
    for m in range(1, GROUP):
        dest = dest + jnp.where(r >= PAIR * m, 1, 0)
    within = r - PAIR * dest
    slot = within - CAP * half
    mine = (slot >= 0) & (slot < CAP) & (r < BLOCK)
    return jnp.where(mine, (z * GROUP + dest) * CAP + slot, -7).astype(F32)


def build_picks(z, tab, p, pick, pick_t, gate_hi, gate_lo, gate_hi_t, gate_lo_t):
    for half in range(2):
        slots = row_slots(z, half)
        ones = jnp.zeros((256, ROWS), F32)
        gates = jnp.zeros((256, ROWS), F32)
        for k in range(TOP):
            hit = tab[2 * p + half, k : k + 1, :] == slots
            ones = jnp.where(hit, 1.0, ones)
            gates = jnp.where(hit, tab[2 * p + half, 8 + k : 9 + k, :], gates)
        hi = gates.astype(BF16).astype(F32)
        lo = gates - hi
        lanes = slice(ROWS * half, ROWS * half + ROWS)
        pick[p, :, lanes] = ones.astype(BF16)
        gate_hi[p, :, lanes] = hi.astype(BF16)
        gate_lo[p, :, lanes] = lo.astype(BF16)
        pick_t[p, lanes, :] = ones.T.astype(BF16)
        gate_hi_t[p, lanes, :] = hi.T.astype(BF16)
        gate_lo_t[p, lanes, :] = lo.T.astype(BF16)


def dispatch(at, rows, zbuf, gbuf, xrecv, sems, before_gather, selectors, experts_of):
    zs, zr, xs, xr = sems

    def up_to(s):
        return (s, 0) if s < 4 else (3, ROWS)

    def plus(s, c):
        src = rows if s == 1 else zbuf.at[s - 1, pl.ds(0, ROWS)]
        p, r = up_to(s)
        return remote(src.at[:, cols(c)], zbuf.at[p, pl.ds(r, ROWS), cols(c)],
                      zs.at[0, s - 1, c], zr.at[0, s - 1, c], at.ring(1))

    def minus(s, c):
        src = rows if s == 1 else zbuf.at[s - 2, pl.ds(ROWS, ROWS)]
        return remote(src.at[:, cols(c)], zbuf.at[s - 1, pl.ds(ROWS, ROWS), cols(c)],
                      zs.at[1, s - 1, c], zr.at[1, s - 1, c], at.ring(-1))

    def has_plus(s, c):
        return s < 4 or (s == 4 and c < 2)

    def has_minus(s, c):
        return s < 4 or (s == 4 and c >= 2)

    for c in range(4):
        plus(1, c).start()
        minus(1, c).start()
    zbuf[0, 0:ROWS, :] = rows[...]
    before_gather()
    for s in range(1, 5):
        p = s - 1
        for c in (0, 1, 2, 3) if s < 4 else (0, 2, 1, 3):
            if has_plus(s, c):
                plus(s, c).wait_recv()
            if has_minus(s, c):
                minus(s, c).wait_recv()
            if s < 4:
                if has_plus(s + 1, c):
                    plus(s + 1, c).start()
                if has_minus(s + 1, c):
                    minus(s + 1, c).start()
            block = zbuf[p, :, c * CHUNK : (c + 1) * CHUNK]
            picked = jnp.zeros((BLOCK, CHUNK), F32)
            for selector in selectors:
                picked = picked + jnp.dot(selector[p, 0:BLOCK, :], block, preferred_element_type=F32)
            gbuf[p, :, :, c * CHUNK : (c + 1) * CHUNK] = picked.astype(BF16).reshape(
                GROUP, PAIR, CHUNK
            )
            for o in range(1, GROUP):
                remote(gbuf.at[p, at.mate(o), :, cols(c)], xrecv.at[p, at.g, :, cols(c)],
                       xs.at[p], xr.at[p], at.group(o)).start()
        xrecv[p, at.g] = gbuf[p, at.g]
        if s >= 2:
            arrive(at, p - 1, gbuf, xrecv, xs, xr)
            experts_of(p - 1)
    arrive(at, 3, gbuf, xrecv, xs, xr)
    for s in range(1, 5):
        for c in range(4):
            if has_plus(s, c):
                plus(s, c).wait_send()
            if has_minus(s, c):
                minus(s, c).wait_send()


def arrive(at, p, gbuf, xrecv, xs, xr):
    whole = remote(gbuf.at[p, pl.ds(0, GROUP - 1)], xrecv.at[p, pl.ds(0, GROUP - 1)],
                   xs.at[p], xr.at[p], at.group(1))
    whole.wait_send()
    whole.wait_recv()


def send_back(at, p, ybuf, crecv, cs, cr):
    for c in (0, 2, 1, 3):
        for o in range(1, GROUP):
            remote(ybuf.at[p, at.mate(o), :, cols(c)], crecv.at[p, at.g, :, cols(c)],
                   cs.at[p, c], cr.at[p, c], at.group(o)).start()
    crecv[p, at.g] = ybuf[p, at.g]


def combine(at, ybuf, crecv, rsend, rrecv, sems, selectors_t, finish):
    cs, cr, rs, rr = sems
    seen = set()

    def partial(p, half, c):
        if (p, c) not in seen:
            seen.add((p, c))
            whole = remote(ybuf.at[p, pl.ds(0, GROUP - 1), :, cols(c)],
                           crecv.at[p, pl.ds(0, GROUP - 1), :, cols(c)],
                           cs.at[p, c], cr.at[p, c], at.group(1))
            whole.wait_send()
            whole.wait_recv()
        block = crecv[p, :, :, c * CHUNK : (c + 1) * CHUNK].reshape(BLOCK, CHUNK)
        total = jnp.zeros((ROWS, CHUNK), F32)
        for selector in selectors_t:
            total = total + jnp.dot(
                selector[p, half * ROWS : (half + 1) * ROWS, 0:BLOCK], block,
                preferred_element_type=F32,
            )
        return total

    def has(way, t, c):
        return t > 1 or (c < 2) == (way == 0)

    def hop(way, t, c):
        return remote(rsend.at[way, t - 1, :, cols(c)], rrecv.at[way, t - 1, :, cols(c)],
                      rs.at[way, t - 1, c], rr.at[way, t - 1, c], at.ring(1 if way == 0 else -1))

    def unit(way, t, c):
        if not has(way, t, c):
            return
        p, half = (4 - t, 1) if way == 0 or t == 1 else (5 - t, 0)
        total = partial(p, half, c)
        window = slice(c * CHUNK, (c + 1) * CHUNK)
        if t > 1 and has(way, t - 1, c):
            hop(way, t - 1, c).wait_recv()
            total = total + rrecv[way, t - 2, :, window].astype(F32)
        rsend[way, t - 1, :, window] = total.astype(BF16)
        hop(way, t, c).start()

    for t in range(1, 5):
        for c in range(4):
            unit(0, t, c if t == 1 else c ^ 2)
            unit(1, t, c)
    for c in range(4):
        total = partial(0, 0, c)
        window = slice(c * CHUNK, (c + 1) * CHUNK)
        for way in range(2):
            hop(way, 4, c).wait_recv()
            total = total + rrecv[way, 3, :, window].astype(F32)
        finish(c, total)
    for t in range(1, 5):
        for c in range(4):
            for way in range(2):
                if has(way, t, c):
                    hop(way, t, c).wait_send()


def forward_kernel(rows, ids_t, gates_t, wg_hbm, wu_hbm, wd_hbm,
                   mixed, tab_out, pick_out, pick_t_out, hi_out, lo_out, gate_out, up_out, back_out,
                   wg, wu, wd, tab, tab_own, pick, pick_t, gate_hi, gate_lo, gate_hi_t, gate_lo_t,
                   zbuf, gbuf, xrecv, hidden, gate_pre, up_pre, ybuf, crecv, rsend, rrecv,
                   zs, zr, xs, xr, cs, cr, rs, rr, ts, tr, ws, os):
    at = Place()
    loads = [pltpu.make_async_copy(a.at[0], b, ws.at[i])
             for i, (a, b) in enumerate(((wg_hbm, wg), (wu_hbm, wu), (wd_hbm, wd)))]
    for load in loads:
        load.start()
    at.barrier()

    def tables():
        tab_own[...] = slot_rows(ids_t[...], gates_t[...])
        tab[0] = tab_own[...]
        sends = [remote(tab_own, tab.at[PLACE[RING - o]], ts.at[o], tr.at[PLACE[RING - o]],
                        at.ring(o)) for o in range(1, RING)]
        for send in sends:
            send.start()
        for send in sends:
            send.wait_recv()
        for p in range(4):
            build_picks(at.z, tab, p, pick, pick_t, gate_hi, gate_lo, gate_hi_t, gate_lo_t)
        for send in sends:
            send.wait_send()

    first = []

    def experts_of(p):
        if not first:
            first.append(1)
            for load in loads:
                load.wait()

        def up_step(n, carry):
            window = pl.ds(pl.multiple_of(n * 256, 256), 256)
            x = xrecv[p].reshape(BLOCK, D)
            a = jnp.dot(x, wg[:, window], preferred_element_type=F32)
            b = jnp.dot(x, wu[:, window], preferred_element_type=F32)
            gate_pre[p, :, window] = a
            up_pre[p, :, window] = b
            hidden[:, window] = (a * jax.nn.sigmoid(a) * b).astype(BF16)
            return carry

        lax.fori_loop(0, FFW // 256, up_step, 0)

        def down_step(n, carry):
            window = pl.ds(pl.multiple_of(n * 256, 256), 256)
            y = jnp.dot(hidden[...], wd[:, window], preferred_element_type=F32)
            ybuf[p, :, :, window] = y.astype(BF16).reshape(GROUP, PAIR, 256)
            return carry

        lax.fori_loop(0, D // 256, down_step, 0)

    dispatch(at, rows, zbuf, gbuf, xrecv, (zs, zr, xs, xr), tables, (pick,), experts_of)
    send_back(at, 2, ybuf, crecv, cs, cr)
    experts_of(3)
    for p in (3, 1, 0):
        send_back(at, p, ybuf, crecv, cs, cr)

    def finish(c, total):
        mixed[:, c * CHUNK : (c + 1) * CHUNK] = total

    combine(at, ybuf, crecv, rsend, rrecv, (cs, cr, rs, rr), (gate_hi_t, gate_lo_t), finish)
    outs = [pltpu.make_async_copy(a, b, os.at[i]) for i, (a, b) in enumerate((
        (tab, tab_out), (pick, pick_out), (pick_t, pick_t_out), (gate_hi, hi_out), (gate_lo, lo_out),
        (gate_pre, gate_out), (up_pre, up_out), (crecv, back_out)))]
    for out in outs:
        out.start()
    for out in outs:
        out.wait()


def backward_kernel(rows, state_grad, tab_hbm, pick_hbm, pick_t_hbm, hi_hbm, lo_hbm, gate_hbm, up_hbm,
                    back_hbm, wg_hbm, wu_hbm, wd_hbm,
                    grad_in, gates_out,
                    wg, wu, wd, tab, pick, pick_t, gate_hi, gate_lo, gate_pre, up_pre, back,
                    zbuf, gbuf, xrecv, hidden, hidden2, ybuf, crecv, rsend, rrecv, dots, dots_recv,
                    zs, zr, xs, xr, cs, cr, rs, rr, ds, dr, ws):
    at = Place()
    loads = [pltpu.make_async_copy(a, b, ws.at[i]) for i, (a, b) in enumerate((
        (tab_hbm, tab), (pick_hbm, pick), (pick_t_hbm, pick_t), (hi_hbm, gate_hi), (lo_hbm, gate_lo),
        (wd_hbm.at[0], wd), (gate_hbm, gate_pre), (up_hbm, up_pre), (wg_hbm.at[0], wg),
        (wu_hbm.at[0], wu), (back_hbm, back)))]
    for load in loads:
        load.start()
    at.barrier()

    def tables():
        for load in loads[:5]:
            load.wait()

    first = []

    def experts_of(p):
        if not first:
            first.append(1)
            for load in loads[5:]:
                load.wait()
        across = (((1,), (1,)), ((), ()))

        def down_step(n, carry):
            window = pl.ds(pl.multiple_of(n * 256, 256), 256)
            x = xrecv[p].reshape(BLOCK, D)
            grad = lax.dot_general(x, wd[window, :], across, preferred_element_type=F32)
            a = gate_pre[p, :, window]
            s = jax.nn.sigmoid(a)
            hidden[:, window] = (grad * up_pre[p, :, window] * (s * (1.0 + a * (1.0 - s)))).astype(BF16)
            hidden2[:, window] = (grad * (a * s)).astype(BF16)
            return carry

        lax.fori_loop(0, FFW // 256, down_step, 0)

        def up_step(n, carry):
            window = pl.ds(pl.multiple_of(n * 256, 256), 256)
            y = lax.dot_general(hidden[...], wg[window, :], across, preferred_element_type=F32)
            y = y + lax.dot_general(hidden2[...], wu[window, :], across, preferred_element_type=F32)
            ybuf[p, :, :, window] = y.astype(BF16).reshape(GROUP, PAIR, 256)
            return carry

        lax.fori_loop(0, D // 256, up_step, 0)

    def gate_dots(p):
        products = lax.dot_general(back[p].reshape(BLOCK, D), zbuf[p], (((1,), (1,)), ((), ())),
                                   preferred_element_type=F32)
        for half in range(2):
            slots = row_slots(at.z, half)[0:BLOCK]
            mine = products[:, ROWS * half : ROWS * half + ROWS]
            picked = [jnp.sum(jnp.where(tab[2 * p + half, k : k + 1, :] == slots, mine, 0.0),
                              axis=0, keepdims=True) for k in range(TOP)]
            dots[2 * p + half] = jnp.concatenate(picked + [jnp.zeros((2, ROWS), F32)], axis=0)

    dispatch(at, rows, zbuf, gbuf, xrecv, (zs, zr, xs, xr), tables, (gate_hi, gate_lo), experts_of)
    send_back(at, 2, ybuf, crecv, cs, cr)
    experts_of(3)
    for p in (3, 1, 0):
        send_back(at, p, ybuf, crecv, cs, cr)
    for p in range(4):
        gate_dots(p)
    dot_sends = [remote(dots.at[PLACE[o]], dots_recv.at[PLACE[RING - o]], ds.at[o],
                        dr.at[PLACE[RING - o]], at.ring(o)) for o in range(1, RING)]
    for send in dot_sends:
        send.start()

    def finish(c, total):
        window = slice(c * CHUNK, (c + 1) * CHUNK)
        grad_in[:, window] = (state_grad[:, window] + total).astype(BF16)

    combine(at, ybuf, crecv, rsend, rrecv, (cs, cr, rs, rr), (pick_t,), finish)
    total = dots[0]
    for o in range(1, RING):
        dot_sends[o - 1].wait_recv()
    for o in range(1, RING):
        total = total + dots_recv[PLACE[RING - o]]
    gates_out[...] = total
    for send in dot_sends:
        send.wait_send()


VMEM = pl.BlockSpec(memory_space=pltpu.VMEM)
ANY = pl.BlockSpec(memory_space=pl.ANY)
DMA = pltpu.SemaphoreType.DMA
SELECTOR = ((4, 256, 256), BF16)
PAIRS = ((4, GROUP, PAIR, D), BF16)
PRES = ((4, BLOCK, FFW), F32)
TABLES = ((RING, 16, ROWS), F32)


def exchange_scratch():
    return dict(
        zbuf=pltpu.VMEM((4, 2 * ROWS, D), BF16), gbuf=pltpu.VMEM(*PAIRS), xrecv=pltpu.VMEM(*PAIRS),
        ybuf=pltpu.VMEM(*PAIRS), crecv=pltpu.VMEM(*PAIRS),
        rsend=pltpu.VMEM((2, 4, ROWS, D), BF16), rrecv=pltpu.VMEM((2, 4, ROWS, D), BF16),
        wg=pltpu.VMEM((D, FFW), BF16), wu=pltpu.VMEM((D, FFW), BF16), wd=pltpu.VMEM((FFW, D), BF16),
        zs=DMA((2, 4, 4)), zr=DMA((2, 4, 4)), xs=DMA((4,)), xr=DMA((4,)), cs=DMA((4, 4)), cr=DMA((4, 4)),
        rs=DMA((2, 4, 4)), rr=DMA((2, 4, 4)),
    )


def run_forward(rows, ids_t, gates_t, wg, wu, wd):
    s = exchange_scratch()
    selector = pltpu.VMEM(*SELECTOR)
    outs = [((ROWS, D), F32), TABLES, SELECTOR, SELECTOR, SELECTOR, SELECTOR, PRES, PRES, PAIRS]
    return pl.pallas_call(
        forward_kernel,
        out_shape=[jax.ShapeDtypeStruct(*o) for o in outs],
        in_specs=[VMEM, VMEM, VMEM, ANY, ANY, ANY],
        out_specs=[VMEM] + [ANY] * 8,
        scratch_shapes=[
            s["wg"], s["wu"], s["wd"], pltpu.VMEM(*TABLES), pltpu.VMEM((16, ROWS), F32),
            selector, selector, selector, selector, selector, selector,
            s["zbuf"], s["gbuf"], s["xrecv"], pltpu.VMEM((BLOCK, FFW), BF16),
            pltpu.VMEM(*PRES), pltpu.VMEM(*PRES), s["ybuf"], s["crecv"], s["rsend"], s["rrecv"],
            s["zs"], s["zr"], s["xs"], s["xr"], s["cs"], s["cr"], s["rs"], s["rr"],
            DMA((RING,)), DMA((RING,)), DMA((3,)), DMA((8,)),
        ],
        compiler_params=pltpu.CompilerParams(
            collective_id=0, has_side_effects=True, vmem_limit_bytes=64 * 1024 * 1024 - 65536
        ),
        name="forward_exchange",
    )(rows, ids_t, gates_t, wg, wu, wd)


def run_backward(rows, state_grad, saved, wg, wu, wd):
    s = exchange_scratch()
    selector = pltpu.VMEM(*SELECTOR)
    return pl.pallas_call(
        backward_kernel,
        out_shape=[jax.ShapeDtypeStruct((ROWS, D), BF16), jax.ShapeDtypeStruct((8, ROWS), F32)],
        in_specs=[VMEM, VMEM] + [ANY] * 11,
        out_specs=[VMEM, VMEM],
        scratch_shapes=[
            s["wg"], s["wu"], s["wd"], pltpu.VMEM(*TABLES), selector, selector, selector, selector,
            pltpu.VMEM(*PRES), pltpu.VMEM(*PRES), pltpu.VMEM(*PAIRS),
            s["zbuf"], s["gbuf"], s["xrecv"], pltpu.VMEM((BLOCK, FFW), BF16), pltpu.VMEM((BLOCK, FFW), BF16),
            s["ybuf"], s["crecv"], s["rsend"], s["rrecv"],
            pltpu.VMEM((RING, 8, ROWS), F32), pltpu.VMEM((RING, 8, ROWS), F32),
            s["zs"], s["zr"], s["xs"], s["xr"], s["cs"], s["cr"], s["rs"], s["rr"],
            DMA((RING,)), DMA((RING,)), DMA((11,)),
        ],
        compiler_params=pltpu.CompilerParams(
            collective_id=1, has_side_effects=True, vmem_limit_bytes=64 * 1024 * 1024 - 65536
        ),
        name="backward_exchange",
    )(rows, state_grad, *saved, wg, wu, wd)


def from_behind(block, axis, distance):
    devices = range(lax.axis_size(axis))
    route = [(i - distance, i) for i in devices if i - distance in devices]
    return lax.ppermute(block, axis, route)


def foot_term(horizon, contact_rep, velocity):
    return foot_weight * horizon[:, None] * contact_rep * velocity


def per_device(
    frames_in,
    expert_ids,
    gate_values,
    gate_weight,
    up_weight,
    down_weight,
    norm_gain,
    pose_weight,
    target_pose,
    foot_contact,
):
    tok_rows, model_width = frames_in.shape
    ep_count = lax.axis_size("ep")
    ids_t = jnp.pad(expert_ids.T, ((0, 2), (0, 0)), constant_values=-1)
    gates_t = jnp.pad(gate_values.T, ((0, 2), (0, 0)))
    mixed_rows, *saved = run_forward(frames_in, ids_t, gates_t, gate_weight, up_weight, down_weight)
    state_rows = frames_in.astype(jnp.float32) + mixed_rows
    inverse_rms = lax.rsqrt(jnp.mean(state_rows * state_rows, axis=1, keepdims=True) + epsilon)
    unit_rows = state_rows * inverse_rms
    normed = (unit_rows * norm_gain).astype(jnp.bfloat16)
    pose_out = jnp.dot(normed, pose_weight, preferred_element_type=jnp.float32)
    pose_cols = pose_out.shape[1]
    device = lax.axis_index("seg") * ep_count + lax.axis_index("ep")
    frames_all = lax.axis_size("seg") * ep_count * tok_rows
    frame_index = device * tok_rows + jnp.arange(tok_rows, dtype=jnp.int32)
    horizon = 0.5 + frame_index.astype(jnp.float32) / (frames_all - 1)
    feet_count = foot_contact.shape[1]
    foot_cols = 3 * feet_count
    foot_pos = pose_out[:, :foot_cols]
    contact_float = foot_contact.astype(jnp.float32)
    contact_rep = jnp.repeat(contact_float, 3, axis=1)
    before = from_behind(foot_pos[tok_rows - 1 :], ("seg", "ep"), 1)
    earlier = jnp.concatenate([before, foot_pos[:-1]], 0)
    velocity = jnp.where((frame_index > 0)[:, None], foot_pos - earlier, 0.0)
    foot_pull = foot_term(horizon, contact_rep, velocity)
    next_pull = from_behind(foot_pull[:1], ("seg", "ep"), -1)
    pose_error = pose_out - target_pose
    local_sum = 0.5 * jnp.sum(horizon[:, None] * pose_error * pose_error) + 0.5 * jnp.sum(
        foot_pull * velocity
    )
    summed = lax.psum(local_sum, ("seg", "ep"))
    loss_value = summed / (frames_all * pose_cols)
    later_pull = jnp.concatenate([foot_pull[1:], next_pull], 0)
    grad_pose = horizon[:, None] * pose_error
    grad_pose = jnp.concatenate(
        [grad_pose[:, :foot_cols] + (foot_pull - later_pull), grad_pose[:, foot_cols:]], 1
    )
    grad_normed = jnp.einsum(
        "tp,dp->td", grad_pose.astype(jnp.bfloat16), pose_weight, preferred_element_type=jnp.float32
    )
    scaled = grad_normed * norm_gain
    grad_state = inverse_rms * (
        scaled - unit_rows * jnp.mean(scaled * unit_rows, axis=1, keepdims=True)
    )
    moe_grad = grad_state.astype(jnp.bfloat16)
    grad_input, grad_gates_t = run_backward(
        moe_grad, grad_state, saved, gate_weight, up_weight, down_weight
    )
    return (grad_input, grad_gates_t[: expert_ids.shape[1]].T, loss_value)


def solution(mesh):
    in_specs = (
        P(("seg", "ep"), None),
        P(("seg", "ep"), None),
        P(("seg", "ep"), None),
        P("ep", None, None),
        P("ep", None, None),
        P("ep", None, None),
        P(),
        P(),
        P(("seg", "ep"), None),
        P(("seg", "ep"), None),
    )
    out_specs = (P(("seg", "ep"), None), P(("seg", "ep"), None), P())
    return jax.shard_map(
        per_device, mesh=mesh, in_specs=in_specs, out_specs=out_specs, check_vma=False
    )
```

time: 651 us -> 353 us (0.54)
  blocking collectives: 350 us -> 80 us
  Pallas kernels: 0 us -> 249 us
  local copies, waits for them, and re-layouts: 113 us -> 5.98 us
  waiting for transfers between devices: 98.1 us -> 1.3 us
  matrix products: 34.2 us -> 3.26 us
  other arithmetic: 23.5 us -> 4 us
  starting transfers between devices: 21.8 us -> 5.64 us
    pallas_call x0 -> x2, Pallas kernels: none -> 249 us  [the longest x1 130 us: run_forward(): pl.pallas_call(forward_kernel, out_shape=[jax.ShapeDtypeStruct(*o) for o...]
    all_to_all x2 -> x0, blocking collectives: 214 us -> none  [the longest x1 108 us: per_device(): lax.all_to_all(send_rows, 'ep', split_axis=0, concat_axis=0, tiled=True)]
    all_to_all x2 -> x0, waiting for transfers between devices: 94.1 us -> none  [the longest x1 94.1 us: per_device(): lax.all_to_all(produced, 'ep', split_axis=0, concat_axis=0, tiled=True)]
    psum x1, blocking collectives: 136 us -> 80 us  [per_device(): summed = lax.psum(local_sum, ('seg', 'ep'))]
    gather x4 -> x0, local copies, waits for them, and re-layouts: 36.5 us -> none  [the longest x1 9.43 us: per_device(): picked = back_flat[position].reshape(tok_rows, top_count, model_width)]
    dot_general x7 -> x0, matrix products: 32.7 us -> none  [the longest x1 6.14 us: per_device(): jnp.einsum('sexd,efd->sexf', grouped, down_weight, preferred_element_type...]
    reshape x5 -> x0, local copies, waits for them, and re-layouts: 30.7 us -> none  [the longest x1 6.25 us: per_device(): picked = back_flat[position].reshape(tok_rows, top_count, model_width)]
    all_to_all x2 -> x0, starting transfers between devices: 14.7 us -> none  [the longest x1 7.38 us: per_device(): lax.all_to_all(produced, 'ep', split_axis=0, concat_axis=0, tiled=True)]
  transfers between devices with their start and end apart: 4 -> 2, of which waited for: 3 -> 2; matrix products, arithmetic and copies ran while one was open for 1% -> 0% of each run, Pallas kernels for 0% -> 0%
where the time goes in v1:
time: 353 us
  Pallas kernels  249 us (71%)
  blocking collectives  80 us (23%)
  local copies, waits for them, and re-layouts  5.98 us (2%)
  starting transfers between devices  5.64 us (2%)
  other arithmetic  4 us (1%)
  between operations  3.9 us (1%)
    pallas_call x1, Pallas kernels, run_forward(): pl.pallas_call(forward_kernel, out_shape=[jax.ShapeDtypeStruct(*o) for o...  130 us
    pallas_call x1, Pallas kernels, run_backward(): pl.pallas_call(backward_kernel, out_shape=[jax.ShapeDtypeStruct((ROWS, D)...  119 us
    psum x1, blocking collectives, per_device(): summed = lax.psum(local_sum, ('seg', 'ep'))  80 us
  transfers between devices with their start and end apart: 2, of which 2 were waited for; matrix products, arithmetic and copies ran while one was open for 0% of the time, Pallas kernels for 0%

profile of v1, /device:TPU:1, one launch (start us, length us, event | category | flops | bytes accessed | tf_op | source)
XLA Modules:
  0.0 353.0 jit_solution(10100829545841421664)
XLA Ops:
  0.6 1.3 pad.8.ids_t
  1.9 1.3 pad.9.gates_t
  3.2 130.1 %forward_exchange.1 = (f32[128,2048]{1,0:T(8,128)}, f32[8,16,128]{2,1,0:T(8,128)}, bf16[4,256,256]{2,1,0:T(8,128)(2,1)}, bf16[4,256,256]{2,1,0:T(8,128)(2,1)}, b...) custom-call(bf16[128,2048]{1,0:T(8,128)(2,1)} %rows.1, ...), custom_call_target="tpu_custom_call" | custom-call | tf_op jit(solution)/shard_map/forward_exchange/pallas_call | solution.py:435
  133.3 0.0 copy-start.4
  133.4 0.0 copy-start
  133.4 0.0 copy-start.1
  133.4 0.0 copy-start.2
  133.4 0.0 copy-start.3
  133.4 1.7 multiply_reduce_fusion.1
  135.2 2.7 multiply_reduce_fusion.2
  137.8 2.3 collective-permute-start
  140.2 0.0 copy-done.4
  140.3 0.1 copy.22
  140.4 0.1 slice.54
  140.5 0.4 collective-permute-done
  140.9 0.7 multiply_reduce_fusion.3
  142.9 80.0 %psum.7 = f32[]{:T(128)} all-reduce(f32[]{:T(128)S(6)} %add.68), channel_id=1, replica_groups=mesh['seg'=4,'ep'=64] {'seg','ep'}, use_global_device_ids=true, to_apply=%region_4.5 | all-reduce | flops 1 | bytes 8 | tf_op jit(solution)/shard_map/psum | solution.py:530
  222.9 3.3 collective-permute-start.1
  226.9 0.9 collective-permute-done.1
  227.8 0.0 copy-done
  227.8 0.0 copy-done.1
  227.8 0.0 copy-done.2
  227.8 0.0 copy-done.3
  227.8 0.6 multiply_reduce_fusion
  228.4 1.5 fusion.10
  229.9 118.8 %backward_exchange.1 = (bf16[128,2048]{1,0:T(8,128)(2,1)}, f32[8,128]{1,0:T(8,128)}) custom-call(bf16[128,2048]{1,0:T(8,128)(2,1)} %get-tuple-element.27.rows, f32[128,2048]{1,0:T(8,128)} %get-tuple-element.28.state_grad, f32[8,16,128]{2,1,0:T(8,128)} %get-tuple-element.15.tab_hbm, bf16[4,256,256]{2,1,0:T(8,128)(2,1)} %get-tuple-element.16.pick_hbm, ...), custom_call_target="tpu_custom_call" | custom-call | tf_op jit(solution)/shard_map/backward_exchange/pallas_call | solution.py:458
  348.7 1.3 slice_bitcast_fusion
  350.0 1.9 copy.24
  (12 shorter events, 0.1 us)
Async XLA Ops:
  133.3 6.9 %copy-start.4 = (s32[128,4]{0,1:T(4,128)S(1)}, s32[128,4]{0,1:T(4,128)}, u32[]{:S(2)}) copy-start(s32[128,4]{0,1:T(4,128)} %param.19) | copy-start | bytes 6148
  133.4 94.4 %copy-start = (f32[128,2048]{1,0:T(8,128)S(1)}, f32[128,2048]{1,0:T(8,128)}, u32[]{:S(2)}) copy-start(f32[128,2048]{1,0:T(8,128)} %get-tuple-element.14) | copy-start | bytes 3145732
  133.4 94.4 %copy-start.1 = (bf16[128,2048]{1,0:T(8,128)(2,1)S(1)}, bf16[128,2048]{1,0:T(8,128)(2,1)}, u32[]{:S(2)}) copy-start(bf16[128,2048]{1,0:T(8,128)(2,1)} %rows.1) | copy-start | bytes 1572868
  133.4 94.4 %copy-start.2 = (bf16[2048,256]{1,0:T(8,128)(2,1)S(1)}, bf16[2048,256]{1,0:T(8,128)(2,1)}, u32[]{:S(2)}) copy-start(bf16[2048,256]{1,0:T(8,128)(2,1)} %param.17) | copy-start | bytes 3145732
  133.4 94.4 %copy-start.3 = (f32[2048]{0:T(1024)S(1)}, f32[2048]{0:T(1024)}, u32[]{:S(2)}) copy-start(f32[2048]{0:T(1024)} %param.16) | copy-start | bytes 24580
  137.8 3.0 collective-permute-start
  222.9 4.8 %collective-permute-start.1 = (f32[1,12]{1,0:T(1,128)S(1)}, f32[1,12]{1,0:T(1,128)S(1)}, u32[]{:S(2)}, u32[]{:S(2)}) collective-permute-start(f32[1,12]{1,0:T(1,128)S(1)} %slice.40), channel_id=1, source_target_pairs={{1,0},{2,1},{3,2},{4,3},{5,4},{6,5},{7,6},{8,7},{9,8},{10,9},{11,1... | collective-permute-start | bytes 152 | tf_op jit(solution)/shard_map/ppermute | solution.py:482

commit v2 on v1

--- a/solution.py
+++ b/solution.py
@@ -1,5 +1,3 @@
-import functools
-
 import jax
 import jax.numpy as jnp
 from jax import lax
@@ -17,6 +15,8 @@
 CAP = 12
 TOP = 6
 D = 2048
+POSE = 256
+FEET = 4
 FFW = 768
 CHUNK = 512
 PAIR = 2 * CAP
@@ -36,6 +36,9 @@
         ep = lax.axis_index("ep")
         self.z = lax.div(ep, GROUP)
         self.g = lax.rem(ep, GROUP)
+        self.seg = lax.axis_index("seg")
+        self.segs = lax.axis_size("seg")
+        self.index = self.seg * (RING * GROUP) + ep
 
     def ring(self, distance):
         return {"ep": lax.rem(self.z + distance + RING, RING) * GROUP + self.g}
@@ -45,6 +48,14 @@
 
     def group(self, offset):
         return {"ep": self.z * GROUP + self.mate(offset)}
+
+    def segment(self, offset):
+        return {"seg": lax.rem(self.seg + offset, self.segs)}
+
+    def next(self, offset):
+        devices = RING * GROUP * self.segs
+        index = lax.rem(self.index + offset + devices, devices)
+        return {"seg": lax.div(index, RING * GROUP), "ep": lax.rem(index, RING * GROUP)}
 
     def barrier(self):
         semaphore = pltpu.get_barrier_semaphore()
@@ -52,7 +63,11 @@
             pl.semaphore_signal(semaphore, inc=1, device_id=self.ring(o), device_id_type=MESH)
         for o in range(1, GROUP):
             pl.semaphore_signal(semaphore, inc=1, device_id=self.group(o), device_id_type=MESH)
-        pl.semaphore_wait(semaphore, RING + GROUP - 2)
+        for o in range(1, self.segs):
+            pl.semaphore_signal(semaphore, inc=1, device_id=self.segment(o), device_id_type=MESH)
+        for o in (-1, 1):
+            pl.semaphore_signal(semaphore, inc=1, device_id=self.next(o), device_id_type=MESH)
+        pl.semaphore_wait(semaphore, RING + GROUP + self.segs - 1)
 
 
 def remote(src, dst, send_sem, recv_sem, device):
@@ -249,20 +264,25 @@
                     hop(way, t, c).wait_send()
 
 
-def forward_kernel(rows, ids_t, gates_t, wg_hbm, wu_hbm, wd_hbm,
-                   mixed, tab_out, pick_out, pick_t_out, hi_out, lo_out, gate_out, up_out, back_out,
-                   wg, wu, wd, tab, tab_own, pick, pick_t, gate_hi, gate_lo, gate_hi_t, gate_lo_t,
-                   zbuf, gbuf, xrecv, hidden, gate_pre, up_pre, ybuf, crecv, rsend, rrecv,
-                   zs, zr, xs, xr, cs, cr, rs, rr, ts, tr, ws, os):
+def step_kernel(rows, ids, gates, wg_hbm, wu_hbm, wd_hbm, gain, pose_weight, target, contact,
+                grad_in, gates_out, loss_out,
+                wg, wu, wd, tab, tab_own, pick, pick_t, gate_hi, gate_lo, gate_hi_t, gate_lo_t,
+                zbuf, gbuf, xrecv, hidden, hidden2, gate_pre, up_pre, ybuf, crecv, crecv2, rsend, rrecv,
+                turn, state, grad_state, moe_grad, foot, foot_recv, tiles, dots, dots_recv,
+                zs, zr, xs, xr, cs, cr, rs, rr, ts, tr, ws, fs, fr, ls, lr, ds, dr):
     at = Place()
     loads = [pltpu.make_async_copy(a.at[0], b, ws.at[i])
              for i, (a, b) in enumerate(((wg_hbm, wg), (wu_hbm, wu), (wd_hbm, wd)))]
     for load in loads:
         load.start()
     at.barrier()
+    across = (((1,), (1,)), ((), ()))
 
     def tables():
-        tab_own[...] = slot_rows(ids_t[...], gates_t[...])
+        turn[...] = jnp.zeros((2, ROWS, ROWS), F32)
+        turn[0, :, 0:TOP] = ids[...].astype(F32)
+        turn[1, :, 0:TOP] = gates[...]
+        tab_own[...] = slot_rows(turn[0].T[0:8], turn[1].T[0:8])
         tab[0] = tab_own[...]
         sends = [remote(tab_own, tab.at[PLACE[RING - o]], ts.at[o], tr.at[PLACE[RING - o]],
                         at.ring(o)) for o in range(1, RING)]
@@ -277,7 +297,7 @@
 
     first = []
 
-    def experts_of(p):
+    def experts_forward(p):
         if not first:
             first.append(1)
             for load in loads:
@@ -303,52 +323,114 @@
 
         lax.fori_loop(0, D // 256, down_step, 0)
 
-    dispatch(at, rows, zbuf, gbuf, xrecv, (zs, zr, xs, xr), tables, (pick,), experts_of)
+    dispatch(at, rows, zbuf, gbuf, xrecv, (zs, zr, xs, xr), tables, (pick,), experts_forward)
     send_back(at, 2, ybuf, crecv, cs, cr)
-    experts_of(3)
+    experts_forward(3)
     for p in (3, 1, 0):
         send_back(at, p, ybuf, crecv, cs, cr)
-
-    def finish(c, total):
-        mixed[:, c * CHUNK : (c + 1) * CHUNK] = total
-
-    combine(at, ybuf, crecv, rsend, rrecv, (cs, cr, rs, rr), (gate_hi_t, gate_lo_t), finish)
-    outs = [pltpu.make_async_copy(a, b, os.at[i]) for i, (a, b) in enumerate((
-        (tab, tab_out), (pick, pick_out), (pick_t, pick_t_out), (gate_hi, hi_out), (gate_lo, lo_out),
-        (gate_pre, gate_out), (up_pre, up_out), (crecv, back_out)))]
-    for out in outs:
-        out.start()
-    for out in outs:
-        out.wait()
-
-
-def backward_kernel(rows, state_grad, tab_hbm, pick_hbm, pick_t_hbm, hi_hbm, lo_hbm, gate_hbm, up_hbm,
-                    back_hbm, wg_hbm, wu_hbm, wd_hbm,
-                    grad_in, gates_out,
-                    wg, wu, wd, tab, pick, pick_t, gate_hi, gate_lo, gate_pre, up_pre, back,
-                    zbuf, gbuf, xrecv, hidden, hidden2, ybuf, crecv, rsend, rrecv, dots, dots_recv,
-                    zs, zr, xs, xr, cs, cr, rs, rr, ds, dr, ws):
-    at = Place()
-    loads = [pltpu.make_async_copy(a, b, ws.at[i]) for i, (a, b) in enumerate((
-        (tab_hbm, tab), (pick_hbm, pick), (pick_t_hbm, pick_t), (hi_hbm, gate_hi), (lo_hbm, gate_lo),
-        (wd_hbm.at[0], wd), (gate_hbm, gate_pre), (up_hbm, up_pre), (wg_hbm.at[0], wg),
-        (wu_hbm.at[0], wu), (back_hbm, back)))]
-    for load in loads:
-        load.start()
-    at.barrier()
-
-    def tables():
-        for load in loads[:5]:
-            load.wait()
-
-    first = []
-
-    def experts_of(p):
-        if not first:
-            first.append(1)
-            for load in loads[5:]:
-                load.wait()
-        across = (((1,), (1,)), ((), ()))
+    squares = []
+
+    def finish_state(c, total):
+        window = slice(c * CHUNK, (c + 1) * CHUNK)
+        sums = rows[:, window].astype(F32) + total
+        state[:, window] = sums
+        squares.append(jnp.sum(sums * sums, axis=1, keepdims=True))
+
+    combine(at, ybuf, crecv, rsend, rrecv, (cs, cr, rs, rr), (gate_hi_t, gate_lo_t), finish_state)
+
+    inverse = lax.rsqrt((squares[0] + squares[1] + squares[2] + squares[3]) / D + epsilon)
+    pose = jnp.zeros((ROWS, POSE), F32)
+    for c in range(4):
+        window = slice(c * CHUNK, (c + 1) * CHUNK)
+        normed = (state[:, window] * inverse * gain[:, window]).astype(BF16)
+        pose = pose + jnp.dot(normed, pose_weight[window, :], preferred_element_type=F32)
+    place = pl.multiple_of(at.index * ROWS, ROWS)
+    frames = lax.broadcasted_iota(jnp.int32, (ROWS, 1), 0) + place
+    frames_all = RING * GROUP * ROWS * at.segs
+    horizon = 0.5 + frames.astype(F32) / (frames_all - 1)
+    lanes = lax.broadcasted_iota(jnp.int32, (ROWS, ROWS), 1)
+    contacts = jnp.zeros((ROWS, ROWS), F32)
+    for k in range(FEET):
+        here = (lanes >= 3 * k) & (lanes < 3 * k + 3)
+        contacts = jnp.where(here, contact[:, k : k + 1].astype(F32), contacts)
+    feet = pose[:, 0:ROWS]
+    foot[0:8, :] = feet[0:8]
+    foot[8:16, :] = contacts[0:8]
+    foot[16:24, :] = feet[ROWS - 8 :]
+    to_next = remote(foot.at[pl.ds(16, 8)], foot_recv.at[pl.ds(16, 8)], fs.at[0], fr.at[0], at.next(1))
+    to_last = remote(foot.at[pl.ds(0, 16)], foot_recv.at[pl.ds(0, 16)], fs.at[1], fr.at[1], at.next(-1))
+    to_next.start()
+    to_last.start()
+    error = pose - target[...]
+    grad_pose = horizon * error
+    grad_far = grad_pose[:, ROWS:].astype(BF16)
+    squared = grad_pose * error
+    grad_parts = [
+        lax.dot_general(grad_far, pose_weight[c * CHUNK : (c + 1) * CHUNK, ROWS:], across,
+                        preferred_element_type=F32) for c in range(4)]
+    for c in range(4):
+        grad_state[:, c * CHUNK : (c + 1) * CHUNK] = grad_parts[c]
+    to_next.wait_recv()
+    to_last.wait_recv()
+    row = lax.broadcasted_iota(jnp.int32, (ROWS, ROWS), 0)
+    earlier = jnp.where(row == 0, foot_recv[23:24, :], pltpu.roll(feet, 1, 0))
+    velocity = jnp.where(frames > 0, feet - earlier, 0.0)
+    pull = foot_weight * horizon * contacts * velocity
+    next_horizon = 0.5 + (place + ROWS).astype(F32) / (frames_all - 1)
+    next_pull = foot_weight * next_horizon * foot_recv[8:9, :] * (foot_recv[0:1, :] - feet[ROWS - 1 :])
+    next_pull = jnp.where(frames[ROWS - 1 :] < frames_all - 1, next_pull, 0.0)
+    later = jnp.where(row == ROWS - 1, next_pull, pltpu.roll(pull, ROWS - 1, 0))
+    terms = squared[:, 0:ROWS] + squared[:, ROWS:] + pull * velocity
+    grad_near = (grad_pose[:, 0:ROWS] + (pull - later)).astype(BF16)
+    products = jnp.zeros((ROWS, 1), F32)
+    for c in range(4):
+        window = slice(c * CHUNK, (c + 1) * CHUNK)
+        grad_normed = grad_state[:, window] + lax.dot_general(
+            grad_near, pose_weight[window, 0:ROWS], across, preferred_element_type=F32
+        )
+        scaled = grad_normed * gain[:, window]
+        grad_state[:, window] = scaled
+        products = products + jnp.sum(scaled * (state[:, window] * inverse), axis=1, keepdims=True)
+    products = products / D
+    for c in range(4):
+        window = slice(c * CHUNK, (c + 1) * CHUNK)
+        grads = inverse * (grad_state[:, window] - state[:, window] * inverse * products)
+        grad_state[:, window] = grads
+        moe_grad[:, window] = grads.astype(BF16)
+    to_next.wait_send()
+    to_last.wait_send()
+
+    tile = jnp.zeros((8, ROWS), F32)
+    for r in range(0, ROWS, 8):
+        tile = tile + terms[r : r + 8]
+
+    def share(stage, here, size, device, value):
+        tiles[stage, here] = value
+        sends = [remote(tiles.at[stage, here], tiles.at[stage, here], ls.at[stage, o], lr.at[stage],
+                        device(o)) for o in range(1, size)]
+        for send in sends:
+            send.start()
+        return sends
+
+    def gather_tile(stage, size, sends):
+        remote(tiles.at[stage, pl.ds(0, size - 1)], tiles.at[stage, pl.ds(0, size - 1)],
+               ls.at[stage, 0], lr.at[stage], at.ring(1)).wait_recv()
+        for send in sends:
+            send.wait_send()
+        total = tiles[stage, 0]
+        for i in range(1, size):
+            total = total + tiles[stage, i]
+        return total
+
+    shares = []
+
+    def experts_backward(p):
+        if p == 0:
+            value = gather_tile(0, RING, shares.pop())
+            shares.append(share(1, at.g, GROUP, at.group, value))
+        if p == 1:
+            value = gather_tile(1, GROUP, shares.pop())
+            shares.append(share(2, at.seg, at.segs, at.segment, value))
 
         def down_step(n, carry):
             window = pl.ds(pl.multiple_of(n * 256, 256), 256)
@@ -372,7 +454,7 @@
         lax.fori_loop(0, D // 256, up_step, 0)
 
     def gate_dots(p):
-        products = lax.dot_general(back[p].reshape(BLOCK, D), zbuf[p], (((1,), (1,)), ((), ())),
+        products = lax.dot_general(crecv[p].reshape(BLOCK, D), zbuf[p], across,
                                    preferred_element_type=F32)
         for half in range(2):
             slots = row_slots(at.z, half)[0:BLOCK]
@@ -381,11 +463,15 @@
                               axis=0, keepdims=True) for k in range(TOP)]
             dots[2 * p + half] = jnp.concatenate(picked + [jnp.zeros((2, ROWS), F32)], axis=0)
 
-    dispatch(at, rows, zbuf, gbuf, xrecv, (zs, zr, xs, xr), tables, (gate_hi, gate_lo), experts_of)
-    send_back(at, 2, ybuf, crecv, cs, cr)
-    experts_of(3)
+    def share_loss():
+        shares.append(share(0, at.z, RING, at.ring, tile))
+
+    dispatch(at, moe_grad, zbuf, gbuf, xrecv, (zs, zr, xs, xr), share_loss, (gate_hi, gate_lo),
+             experts_backward)
+    send_back(at, 2, ybuf, crecv2, cs, cr)
+    experts_backward(3)
     for p in (3, 1, 0):
-        send_back(at, p, ybuf, crecv, cs, cr)
+        send_back(at, p, ybuf, crecv2, cs, cr)
     for p in range(4):
         gate_dots(p)
     dot_sends = [remote(dots.at[PLACE[o]], dots_recv.at[PLACE[RING - o]], ds.at[o],
@@ -393,14 +479,16 @@
     for send in dot_sends:
         send.start()
 
-    def finish(c, total):
-        window = slice(c * CHUNK, (c + 1) * CHUNK)
-        grad_in[:, window] = (state_grad[:, window] + total).astype(BF16)
-
-    combine(at, ybuf, crecv, rsend, rrecv, (cs, cr, rs, rr), (pick_t,), finish)
+    def finish_input(c, total):
+        window = slice(c * CHUNK, (c + 1) * CHUNK)
+        grad_in[:, window] = (grad_state[:, window] + total).astype(BF16)
+
+    combine(at, ybuf, crecv2, rsend, rrecv, (cs, cr, rs, rr), (pick_t,), finish_input)
+    loss = gather_tile(2, at.segs, shares.pop())
+    loss_out[0, 0] = jnp.sum(loss) * (0.5 / (frames_all * POSE))
+    for send in dot_sends:
+        send.wait_recv()
     total = dots[0]
-    for o in range(1, RING):
-        dot_sends[o - 1].wait_recv()
     for o in range(1, RING):
         total = total + dots_recv[PLACE[RING - o]]
     gates_out[...] = total
@@ -409,81 +497,9 @@
 
 
 VMEM = pl.BlockSpec(memory_space=pltpu.VMEM)
+SMEM = pl.BlockSpec(memory_space=pltpu.SMEM)
 ANY = pl.BlockSpec(memory_space=pl.ANY)
 DMA = pltpu.SemaphoreType.DMA
-SELECTOR = ((4, 256, 256), BF16)
-PAIRS = ((4, GROUP, PAIR, D), BF16)
-PRES = ((4, BLOCK, FFW), F32)
-TABLES = ((RING, 16, ROWS), F32)
-
-
-def exchange_scratch():
-    return dict(
-        zbuf=pltpu.VMEM((4, 2 * ROWS, D), BF16), gbuf=pltpu.VMEM(*PAIRS), xrecv=pltpu.VMEM(*PAIRS),
-        ybuf=pltpu.VMEM(*PAIRS), crecv=pltpu.VMEM(*PAIRS),
-        rsend=pltpu.VMEM((2, 4, ROWS, D), BF16), rrecv=pltpu.VMEM((2, 4, ROWS, D), BF16),
-        wg=pltpu.VMEM((D, FFW), BF16), wu=pltpu.VMEM((D, FFW), BF16), wd=pltpu.VMEM((FFW, D), BF16),
-        zs=DMA((2, 4, 4)), zr=DMA((2, 4, 4)), xs=DMA((4,)), xr=DMA((4,)), cs=DMA((4, 4)), cr=DMA((4, 4)),
-        rs=DMA((2, 4, 4)), rr=DMA((2, 4, 4)),
-    )
-
-
-def run_forward(rows, ids_t, gates_t, wg, wu, wd):
-    s = exchange_scratch()
-    selector = pltpu.VMEM(*SELECTOR)
-    outs = [((ROWS, D), F32), TABLES, SELECTOR, SELECTOR, SELECTOR, SELECTOR, PRES, PRES, PAIRS]
-    return pl.pallas_call(
-        forward_kernel,
-        out_shape=[jax.ShapeDtypeStruct(*o) for o in outs],
-        in_specs=[VMEM, VMEM, VMEM, ANY, ANY, ANY],
-        out_specs=[VMEM] + [ANY] * 8,
-        scratch_shapes=[
-            s["wg"], s["wu"], s["wd"], pltpu.VMEM(*TABLES), pltpu.VMEM((16, ROWS), F32),
-            selector, selector, selector, selector, selector, selector,
-            s["zbuf"], s["gbuf"], s["xrecv"], pltpu.VMEM((BLOCK, FFW), BF16),
-            pltpu.VMEM(*PRES), pltpu.VMEM(*PRES), s["ybuf"], s["crecv"], s["rsend"], s["rrecv"],
-            s["zs"], s["zr"], s["xs"], s["xr"], s["cs"], s["cr"], s["rs"], s["rr"],
-            DMA((RING,)), DMA((RING,)), DMA((3,)), DMA((8,)),
-        ],
-        compiler_params=pltpu.CompilerParams(
-            collective_id=0, has_side_effects=True, vmem_limit_bytes=64 * 1024 * 1024 - 65536
-        ),
-        name="forward_exchange",
-    )(rows, ids_t, gates_t, wg, wu, wd)
-
-
-def run_backward(rows, state_grad, saved, wg, wu, wd):
-    s = exchange_scratch()
-    selector = pltpu.VMEM(*SELECTOR)
-    return pl.pallas_call(
-        backward_kernel,
-        out_shape=[jax.ShapeDtypeStruct((ROWS, D), BF16), jax.ShapeDtypeStruct((8, ROWS), F32)],
-        in_specs=[VMEM, VMEM] + [ANY] * 11,
-        out_specs=[VMEM, VMEM],
-        scratch_shapes=[
-            s["wg"], s["wu"], s["wd"], pltpu.VMEM(*TABLES), selector, selector, selector, selector,
-            pltpu.VMEM(*PRES), pltpu.VMEM(*PRES), pltpu.VMEM(*PAIRS),
-            s["zbuf"], s["gbuf"], s["xrecv"], pltpu.VMEM((BLOCK, FFW), BF16), pltpu.VMEM((BLOCK, FFW), BF16),
-            s["ybuf"], s["crecv"], s["rsend"], s["rrecv"],
-            pltpu.VMEM((RING, 8, ROWS), F32), pltpu.VMEM((RING, 8, ROWS), F32),
-            s["zs"], s["zr"], s["xs"], s["xr"], s["cs"], s["cr"], s["rs"], s["rr"],
-            DMA((RING,)), DMA((RING,)), DMA((11,)),
-        ],
-        compiler_params=pltpu.CompilerParams(
-            collective_id=1, has_side_effects=True, vmem_limit_bytes=64 * 1024 * 1024 - 65536
-        ),
-        name="backward_exchange",
-    )(rows, state_grad, *saved, wg, wu, wd)
-
-
-def from_behind(block, axis, distance):
-    devices = range(lax.axis_size(axis))
-    route = [(i - distance, i) for i in devices if i - distance in devices]
-    return lax.ppermute(block, axis, route)
-
-
-def foot_term(horizon, contact_rep, velocity):
-    return foot_weight * horizon[:, None] * contact_rep * velocity
 
 
 def per_device(
@@ -498,54 +514,43 @@
     target_pose,
     foot_contact,
 ):
-    tok_rows, model_width = frames_in.shape
-    ep_count = lax.axis_size("ep")
-    ids_t = jnp.pad(expert_ids.T, ((0, 2), (0, 0)), constant_values=-1)
-    gates_t = jnp.pad(gate_values.T, ((0, 2), (0, 0)))
-    mixed_rows, *saved = run_forward(frames_in, ids_t, gates_t, gate_weight, up_weight, down_weight)
-    state_rows = frames_in.astype(jnp.float32) + mixed_rows
-    inverse_rms = lax.rsqrt(jnp.mean(state_rows * state_rows, axis=1, keepdims=True) + epsilon)
-    unit_rows = state_rows * inverse_rms
-    normed = (unit_rows * norm_gain).astype(jnp.bfloat16)
-    pose_out = jnp.dot(normed, pose_weight, preferred_element_type=jnp.float32)
-    pose_cols = pose_out.shape[1]
-    device = lax.axis_index("seg") * ep_count + lax.axis_index("ep")
-    frames_all = lax.axis_size("seg") * ep_count * tok_rows
-    frame_index = device * tok_rows + jnp.arange(tok_rows, dtype=jnp.int32)
-    horizon = 0.5 + frame_index.astype(jnp.float32) / (frames_all - 1)
-    feet_count = foot_contact.shape[1]
-    foot_cols = 3 * feet_count
-    foot_pos = pose_out[:, :foot_cols]
-    contact_float = foot_contact.astype(jnp.float32)
-    contact_rep = jnp.repeat(contact_float, 3, axis=1)
-    before = from_behind(foot_pos[tok_rows - 1 :], ("seg", "ep"), 1)
-    earlier = jnp.concatenate([before, foot_pos[:-1]], 0)
-    velocity = jnp.where((frame_index > 0)[:, None], foot_pos - earlier, 0.0)
-    foot_pull = foot_term(horizon, contact_rep, velocity)
-    next_pull = from_behind(foot_pull[:1], ("seg", "ep"), -1)
-    pose_error = pose_out - target_pose
-    local_sum = 0.5 * jnp.sum(horizon[:, None] * pose_error * pose_error) + 0.5 * jnp.sum(
-        foot_pull * velocity
-    )
-    summed = lax.psum(local_sum, ("seg", "ep"))
-    loss_value = summed / (frames_all * pose_cols)
-    later_pull = jnp.concatenate([foot_pull[1:], next_pull], 0)
-    grad_pose = horizon[:, None] * pose_error
-    grad_pose = jnp.concatenate(
-        [grad_pose[:, :foot_cols] + (foot_pull - later_pull), grad_pose[:, foot_cols:]], 1
-    )
-    grad_normed = jnp.einsum(
-        "tp,dp->td", grad_pose.astype(jnp.bfloat16), pose_weight, preferred_element_type=jnp.float32
-    )
-    scaled = grad_normed * norm_gain
-    grad_state = inverse_rms * (
-        scaled - unit_rows * jnp.mean(scaled * unit_rows, axis=1, keepdims=True)
-    )
-    moe_grad = grad_state.astype(jnp.bfloat16)
-    grad_input, grad_gates_t = run_backward(
-        moe_grad, grad_state, saved, gate_weight, up_weight, down_weight
-    )
-    return (grad_input, grad_gates_t[: expert_ids.shape[1]].T, loss_value)
+    segs = lax.axis_size("seg")
+    selector = pltpu.VMEM((4, 256, 256), BF16)
+    pairs = pltpu.VMEM((4, GROUP, PAIR, D), BF16)
+    hidden = pltpu.VMEM((BLOCK, FFW), BF16)
+    pres = pltpu.VMEM((4, BLOCK, FFW), F32)
+    hops = pltpu.VMEM((2, 4, ROWS, D), BF16)
+    wide = pltpu.VMEM((ROWS, D), F32)
+    dots = pltpu.VMEM((RING, 8, ROWS), F32)
+    grad_input, gates_t, loss = pl.pallas_call(
+        step_kernel,
+        out_shape=[
+            jax.ShapeDtypeStruct((ROWS, D), BF16),
+            jax.ShapeDtypeStruct((8, ROWS), F32),
+            jax.ShapeDtypeStruct((1, 1), F32),
+        ],
+        in_specs=[VMEM, VMEM, VMEM, ANY, ANY, ANY, VMEM, VMEM, VMEM, VMEM],
+        out_specs=[VMEM, VMEM, SMEM],
+        scratch_shapes=[
+            pltpu.VMEM((D, FFW), BF16), pltpu.VMEM((D, FFW), BF16), pltpu.VMEM((FFW, D), BF16),
+            pltpu.VMEM((RING, 16, ROWS), F32), pltpu.VMEM((16, ROWS), F32),
+            selector, selector, selector, selector, selector, selector,
+            pltpu.VMEM((4, 2 * ROWS, D), BF16), pairs, pairs, hidden, hidden, pres, pres,
+            pairs, pairs, pairs, hops, hops,
+            pltpu.VMEM((2, ROWS, ROWS), F32), wide, wide, pltpu.VMEM((ROWS, D), BF16),
+            pltpu.VMEM((24, ROWS), F32), pltpu.VMEM((24, ROWS), F32),
+            pltpu.VMEM((3, 8, 8, ROWS), F32), dots, dots,
+            DMA((2, 4, 4)), DMA((2, 4, 4)), DMA((4,)), DMA((4,)), DMA((4, 4)), DMA((4, 4)),
+            DMA((2, 4, 4)), DMA((2, 4, 4)), DMA((RING,)), DMA((RING,)), DMA((3,)),
+            DMA((2,)), DMA((2,)), DMA((3, 8)), DMA((3,)), DMA((RING,)), DMA((RING,)),
+        ],
+        compiler_params=pltpu.CompilerParams(
+            collective_id=0, has_side_effects=True, vmem_limit_bytes=64 * 1024 * 1024 - 65536
+        ),
+        name="step",
+    )(frames_in, expert_ids, gate_values, gate_weight, up_weight, down_weight,
+      norm_gain.reshape(1, D), pose_weight, target_pose, foot_contact)
+    return (grad_input, gates_t[:TOP].T, loss[0, 0])
 
 
 def solution(mesh):

time: 353 us -> 252 us (0.71)
  blocking collectives: 80 us -> 0 us
  Pallas kernels: 249 us -> 242 us
  starting transfers between devices: 5.64 us -> 0 us
  other arithmetic: 4 us -> 0 us
    psum x1 -> x0, blocking collectives: 80 us -> none  [per_device(): summed = lax.psum(local_sum, ('seg', 'ep'))]
    pallas_call x2 -> x1, Pallas kernels: 249 us -> 242 us  [per_device(): pl.pallas_call(step_kernel, out_shape=[jax.ShapeDtypeStruct((ROWS, D), BF...]
    ppermute x2 -> x0, starting transfers between devices: 5.64 us -> none  [from_behind(): return lax.ppermute(block, axis, route)]
    unnamed x11 -> x4, local copies, waits for them, and re-layouts: 1.91 us -> 6.15 us
  transfers between devices with their start and end apart: 2 -> 0, of which waited for: 2 -> 0; matrix products, arithmetic and copies ran while one was open for 0% -> 0% of each run, Pallas kernels for 0% -> 0%
where the time goes in v2:
time: 252 us
  Pallas kernels  242 us (96%)
  local copies, waits for them, and re-layouts  7.42 us (3%)
    pallas_call x1, Pallas kernels, per_device(): pl.pallas_call(step_kernel, out_shape=[jax.ShapeDtypeStruct((ROWS, D), BF...  242 us
    unnamed x4, local copies, waits for them, and re-layouts  6.15 us

profile of v2, /device:TPU:1, one launch (start us, length us, event | category | flops | bytes accessed | tf_op | source)
XLA Modules:
  0.0 252.0 jit_solution(7389051481927015277)
XLA Ops:
  0.6 1.4 copy.13.ids
  2.1 1.4 copy.14.gates
  3.5 1.4 copy.15.contact
  4.9 242.1 %step.1 = (bf16[128,2048]{1,0:T(8,128)(2,1)}, f32[8,128]{1,0:T(8,128)}, f32[1,1]{1,0:T(1,128)}) custom-call(bf16[128,2048]{1,0:T(8,128)(2,1)} %rows.1, s32[128,6]{1,0:T(8,128)} %copy.13.ids, f32[128,6]{1,0:T(8,128)} %copy.14.gates, bf16[1,2048,768]{2,1,0:T(8,128)(2,1)} %wg_hbm.1, bf16[1,2048,768]{2,1,0:T(8,128)(2,1)} %wu_hbm.1, ...), custom_call_target="tpu_custom_call" | custom-call | tf_op jit(solution)/shard_map/step/pallas_call | solution.py:525
  247.0 1.3 slice_bitcast_fusion
  248.3 1.9 copy.18

commit v3 on v2

--- a/solution.py
+++ b/solution.py
@@ -59,7 +59,7 @@
 
     def barrier(self):
         semaphore = pltpu.get_barrier_semaphore()
-        for o in range(1, RING):
+        for o in (-1, 1):
             pl.semaphore_signal(semaphore, inc=1, device_id=self.ring(o), device_id_type=MESH)
         for o in range(1, GROUP):
             pl.semaphore_signal(semaphore, inc=1, device_id=self.group(o), device_id_type=MESH)
@@ -67,7 +67,7 @@
             pl.semaphore_signal(semaphore, inc=1, device_id=self.segment(o), device_id_type=MESH)
         for o in (-1, 1):
             pl.semaphore_signal(semaphore, inc=1, device_id=self.next(o), device_id_type=MESH)
-        pl.semaphore_wait(semaphore, RING + GROUP + self.segs - 1)
+        pl.semaphore_wait(semaphore, GROUP + self.segs + 2)
 
 
 def remote(src, dst, send_sem, recv_sem, device):
@@ -77,7 +77,7 @@
     )
 
 
-def slot_rows(ids_t, gates_t):
+def slot_rows(ids_t):
     experts = lax.broadcasted_iota(jnp.int32, (RING * GROUP, ROWS), 0)
     chosen = jnp.zeros((RING * GROUP, ROWS), F32)
     for k in range(TOP):
@@ -93,8 +93,7 @@
         ids = ids_t[k : k + 1, :]
         rank = jnp.sum(jnp.where(ids == experts, earlier, 0.0), axis=0, keepdims=True)
         table.append(jnp.where(rank < CAP, ids.astype(F32) * CAP + rank, -1.0))
-    table.append(jnp.full((2, ROWS), -1.0, F32))
-    return jnp.concatenate(table + [gates_t], axis=0)
+    return jnp.concatenate(table, axis=0)
 
 
 def row_slots(z, half):
@@ -128,7 +127,7 @@
         gate_lo_t[p, lanes, :] = lo.T.astype(BF16)
 
 
-def dispatch(at, rows, zbuf, gbuf, xrecv, sems, before_gather, selectors, experts_of):
+def dispatch(at, rows, zbuf, gbuf, xrecv, sems, tables, prepare, selectors, experts_of):
     zs, zr, xs, xr = sems
 
     def up_to(s):
@@ -151,14 +150,32 @@
     def has_minus(s, c):
         return s < 4 or (s == 4 and c >= 2)
 
+    def table_copies(s):
+        if not tables:
+            return []
+        tab, ts, tr = tables
+        j = (RING - s + 1) % RING
+        copies = [remote(tab.at[PLACE[j]], tab.at[PLACE[RING - s]], ts.at[0, s - 1], tr.at[0, s - 1],
+                         at.ring(1))]
+        if s < 4:
+            copies.append(remote(tab.at[PLACE[s - 1]], tab.at[PLACE[s]], ts.at[1, s - 1],
+                                 tr.at[1, s - 1], at.ring(-1)))
+        return copies
+
+    for copy in table_copies(1):
+        copy.start()
     for c in range(4):
         plus(1, c).start()
         minus(1, c).start()
     zbuf[0, 0:ROWS, :] = rows[...]
-    before_gather()
     for s in range(1, 5):
         p = s - 1
-        for c in (0, 1, 2, 3) if s < 4 else (0, 2, 1, 3):
+        for copy in table_copies(s):
+            copy.wait_recv()
+        if s < 4:
+            for copy in table_copies(s + 1):
+                copy.start()
+        for i, c in enumerate((0, 1, 2, 3) if s < 4 else (0, 2, 1, 3)):
             if has_plus(s, c):
                 plus(s, c).wait_recv()
             if has_minus(s, c):
@@ -168,6 +185,8 @@
                     plus(s + 1, c).start()
                 if has_minus(s + 1, c):
                     minus(s + 1, c).start()
+            if i == 0:
+                prepare(p)
             block = zbuf[p, :, c * CHUNK : (c + 1) * CHUNK]
             picked = jnp.zeros((BLOCK, CHUNK), F32)
             for selector in selectors:
@@ -184,6 +203,8 @@
             experts_of(p - 1)
     arrive(at, 3, gbuf, xrecv, xs, xr)
     for s in range(1, 5):
+        for copy in table_copies(s):
+            copy.wait_send()
         for c in range(4):
             if has_plus(s, c):
                 plus(s, c).wait_send()
@@ -198,21 +219,31 @@
     whole.wait_recv()
 
 
-def send_back(at, p, ybuf, crecv, cs, cr):
-    for c in (0, 2, 1, 3):
-        for o in range(1, GROUP):
-            remote(ybuf.at[p, at.mate(o), :, cols(c)], crecv.at[p, at.g, :, cols(c)],
-                   cs.at[p, c], cr.at[p, c], at.group(o)).start()
-    crecv[p, at.g] = ybuf[p, at.g]
-
-
-def combine(at, ybuf, crecv, rsend, rrecv, sems, selectors_t, finish):
+BACK_ORDER = [(3, 0), (3, 2), (3, 1), (3, 3)] + [(p, c) for p in (2, 1, 0) for c in (2, 3, 0, 1)]
+AHEAD = 6
+
+
+def combine(at, ybuf, crecv, rsend, rrecv, sems, selectors_t, between, finish):
     cs, cr, rs, rr = sems
     seen = set()
+    waiting = list(BACK_ORDER)
+
+    def send_back():
+        if waiting:
+            p, c = waiting.pop(0)
+            for o in range(1, GROUP):
+                remote(ybuf.at[p, at.mate(o), :, cols(c)], crecv.at[p, at.g, :, cols(c)],
+                       cs.at[p, c], cr.at[p, c], at.group(o)).start()
+            window = slice(c * CHUNK, (c + 1) * CHUNK)
+            crecv[p, at.g, :, window] = ybuf[p, at.g, :, window]
+
+    for i in range(AHEAD):
+        send_back()
 
     def partial(p, half, c):
         if (p, c) not in seen:
             seen.add((p, c))
+            send_back()
             whole = remote(ybuf.at[p, pl.ds(0, GROUP - 1), :, cols(c)],
                            crecv.at[p, pl.ds(0, GROUP - 1), :, cols(c)],
                            cs.at[p, c], cr.at[p, c], at.group(1))
@@ -248,8 +279,10 @@
 
     for t in range(1, 5):
         for c in range(4):
+            c = c if t > 1 else (0, 2, 1, 3)[c]
             unit(0, t, c if t == 1 else c ^ 2)
             unit(1, t, c)
+        between(t)
     for c in range(4):
         total = partial(0, 0, c)
         window = slice(c * CHUNK, (c + 1) * CHUNK)
@@ -266,7 +299,7 @@
 
 def step_kernel(rows, ids, gates, wg_hbm, wu_hbm, wd_hbm, gain, pose_weight, target, contact,
                 grad_in, gates_out, loss_out,
-                wg, wu, wd, tab, tab_own, pick, pick_t, gate_hi, gate_lo, gate_hi_t, gate_lo_t,
+                wg, wu, wd, tab, pick, pick_t, gate_hi, gate_lo, gate_hi_t, gate_lo_t,
                 zbuf, gbuf, xrecv, hidden, hidden2, gate_pre, up_pre, ybuf, crecv, crecv2, rsend, rrecv,
                 turn, state, grad_state, moe_grad, foot, foot_recv, tiles, dots, dots_recv,
                 zs, zr, xs, xr, cs, cr, rs, rr, ts, tr, ws, fs, fr, ls, lr, ds, dr):
@@ -275,25 +308,24 @@
              for i, (a, b) in enumerate(((wg_hbm, wg), (wu_hbm, wu), (wd_hbm, wd)))]
     for load in loads:
         load.start()
+    tab_own = tab.at[0]
+    tab_own[...] = jnp.zeros((16, ROWS), F32)
+    tab_own[0:TOP, :] = slot_rows(ids[...])
+    tab_own[8 : 8 + TOP, :] = gates[...]
+    turn[...] = jnp.zeros((ROWS, ROWS), F32)
+    turn[0:FEET, :] = contact[...].astype(F32)
+    contact_columns = turn[...].T
+    lanes = lax.broadcasted_iota(jnp.int32, (ROWS, ROWS), 1)
+    contacts = jnp.zeros((ROWS, ROWS), F32)
+    for k in range(FEET):
+        here = (lanes >= 3 * k) & (lanes < 3 * k + 3)
+        contacts = jnp.where(here, contact_columns[:, k : k + 1], contacts)
+    turn[...] = contacts
     at.barrier()
     across = (((1,), (1,)), ((), ()))
 
-    def tables():
-        turn[...] = jnp.zeros((2, ROWS, ROWS), F32)
-        turn[0, :, 0:TOP] = ids[...].astype(F32)
-        turn[1, :, 0:TOP] = gates[...]
-        tab_own[...] = slot_rows(turn[0].T[0:8], turn[1].T[0:8])
-        tab[0] = tab_own[...]
-        sends = [remote(tab_own, tab.at[PLACE[RING - o]], ts.at[o], tr.at[PLACE[RING - o]],
-                        at.ring(o)) for o in range(1, RING)]
-        for send in sends:
-            send.start()
-        for send in sends:
-            send.wait_recv()
-        for p in range(4):
-            build_picks(at.z, tab, p, pick, pick_t, gate_hi, gate_lo, gate_hi_t, gate_lo_t)
-        for send in sends:
-            send.wait_send()
+    def picks(p):
+        build_picks(at.z, tab, p, pick, pick_t, gate_hi, gate_lo, gate_hi_t, gate_lo_t)
 
     first = []
 
@@ -323,11 +355,9 @@
 
         lax.fori_loop(0, D // 256, down_step, 0)
 
-    dispatch(at, rows, zbuf, gbuf, xrecv, (zs, zr, xs, xr), tables, (pick,), experts_forward)
-    send_back(at, 2, ybuf, crecv, cs, cr)
+    dispatch(at, rows, zbuf, gbuf, xrecv, (zs, zr, xs, xr), (tab, ts, tr), picks, (pick,),
+             experts_forward)
     experts_forward(3)
-    for p in (3, 1, 0):
-        send_back(at, p, ybuf, crecv, cs, cr)
     squares = []
 
     def finish_state(c, total):
@@ -336,7 +366,8 @@
         state[:, window] = sums
         squares.append(jnp.sum(sums * sums, axis=1, keepdims=True))
 
-    combine(at, ybuf, crecv, rsend, rrecv, (cs, cr, rs, rr), (gate_hi_t, gate_lo_t), finish_state)
+    combine(at, ybuf, crecv, rsend, rrecv, (cs, cr, rs, rr), (gate_hi_t, gate_lo_t),
+            lambda t: None, finish_state)
 
     inverse = lax.rsqrt((squares[0] + squares[1] + squares[2] + squares[3]) / D + epsilon)
     pose = jnp.zeros((ROWS, POSE), F32)
@@ -348,11 +379,7 @@
     frames = lax.broadcasted_iota(jnp.int32, (ROWS, 1), 0) + place
     frames_all = RING * GROUP * ROWS * at.segs
     horizon = 0.5 + frames.astype(F32) / (frames_all - 1)
-    lanes = lax.broadcasted_iota(jnp.int32, (ROWS, ROWS), 1)
-    contacts = jnp.zeros((ROWS, ROWS), F32)
-    for k in range(FEET):
-        here = (lanes >= 3 * k) & (lanes < 3 * k + 3)
-        contacts = jnp.where(here, contact[:, k : k + 1].astype(F32), contacts)
+    contacts = turn[...]
     feet = pose[:, 0:ROWS]
     foot[0:8, :] = feet[0:8]
     foot[8:16, :] = contacts[0:8]
@@ -452,6 +479,8 @@
             return carry
 
         lax.fori_loop(0, D // 256, up_step, 0)
+        if p < 3:
+            gate_dots(p)
 
     def gate_dots(p):
         products = lax.dot_general(crecv[p].reshape(BLOCK, D), zbuf[p], across,
@@ -463,27 +492,27 @@
                               axis=0, keepdims=True) for k in range(TOP)]
             dots[2 * p + half] = jnp.concatenate(picked + [jnp.zeros((2, ROWS), F32)], axis=0)
 
-    def share_loss():
-        shares.append(share(0, at.z, RING, at.ring, tile))
-
-    dispatch(at, moe_grad, zbuf, gbuf, xrecv, (zs, zr, xs, xr), share_loss, (gate_hi, gate_lo),
+    def share_loss(p):
+        if p == 0:
+            shares.append(share(0, at.z, RING, at.ring, tile))
+
+    dispatch(at, moe_grad, zbuf, gbuf, xrecv, (zs, zr, xs, xr), None, share_loss, (gate_hi, gate_lo),
              experts_backward)
-    send_back(at, 2, ybuf, crecv2, cs, cr)
     experts_backward(3)
-    for p in (3, 1, 0):
-        send_back(at, p, ybuf, crecv2, cs, cr)
-    for p in range(4):
-        gate_dots(p)
     dot_sends = [remote(dots.at[PLACE[o]], dots_recv.at[PLACE[RING - o]], ds.at[o],
                         dr.at[PLACE[RING - o]], at.ring(o)) for o in range(1, RING)]
-    for send in dot_sends:
-        send.start()
+
+    def last_dots(t):
+        if t == 1:
+            gate_dots(3)
+            for send in dot_sends:
+                send.start()
 
     def finish_input(c, total):
         window = slice(c * CHUNK, (c + 1) * CHUNK)
         grad_in[:, window] = (grad_state[:, window] + total).astype(BF16)
 
-    combine(at, ybuf, crecv2, rsend, rrecv, (cs, cr, rs, rr), (pick_t,), finish_input)
+    combine(at, ybuf, crecv2, rsend, rrecv, (cs, cr, rs, rr), (pick_t,), last_dots, finish_input)
     loss = gather_tile(2, at.segs, shares.pop())
     loss_out[0, 0] = jnp.sum(loss) * (0.5 / (frames_all * POSE))
     for send in dot_sends:
@@ -491,7 +520,7 @@
     total = dots[0]
     for o in range(1, RING):
         total = total + dots_recv[PLACE[RING - o]]
-    gates_out[...] = total
+    gates_out[...] = total[0:TOP]
     for send in dot_sends:
         send.wait_send()
 
@@ -526,31 +555,31 @@
         step_kernel,
         out_shape=[
             jax.ShapeDtypeStruct((ROWS, D), BF16),
-            jax.ShapeDtypeStruct((8, ROWS), F32),
+            jax.ShapeDtypeStruct((TOP, ROWS), F32),
             jax.ShapeDtypeStruct((1, 1), F32),
         ],
         in_specs=[VMEM, VMEM, VMEM, ANY, ANY, ANY, VMEM, VMEM, VMEM, VMEM],
         out_specs=[VMEM, VMEM, SMEM],
         scratch_shapes=[
             pltpu.VMEM((D, FFW), BF16), pltpu.VMEM((D, FFW), BF16), pltpu.VMEM((FFW, D), BF16),
-            pltpu.VMEM((RING, 16, ROWS), F32), pltpu.VMEM((16, ROWS), F32),
+            pltpu.VMEM((RING, 16, ROWS), F32),
             selector, selector, selector, selector, selector, selector,
             pltpu.VMEM((4, 2 * ROWS, D), BF16), pairs, pairs, hidden, hidden, pres, pres,
             pairs, pairs, pairs, hops, hops,
-            pltpu.VMEM((2, ROWS, ROWS), F32), wide, wide, pltpu.VMEM((ROWS, D), BF16),
+            pltpu.VMEM((ROWS, ROWS), F32), wide, wide, pltpu.VMEM((ROWS, D), BF16),
             pltpu.VMEM((24, ROWS), F32), pltpu.VMEM((24, ROWS), F32),
             pltpu.VMEM((3, 8, 8, ROWS), F32), dots, dots,
             DMA((2, 4, 4)), DMA((2, 4, 4)), DMA((4,)), DMA((4,)), DMA((4, 4)), DMA((4, 4)),
-            DMA((2, 4, 4)), DMA((2, 4, 4)), DMA((RING,)), DMA((RING,)), DMA((3,)),
+            DMA((2, 4, 4)), DMA((2, 4, 4)), DMA((2, 4)), DMA((2, 4)), DMA((3,)),
             DMA((2,)), DMA((2,)), DMA((3, 8)), DMA((3,)), DMA((RING,)), DMA((RING,)),
         ],
         compiler_params=pltpu.CompilerParams(
             collective_id=0, has_side_effects=True, vmem_limit_bytes=64 * 1024 * 1024 - 65536
         ),
         name="step",
-    )(frames_in, expert_ids, gate_values, gate_weight, up_weight, down_weight,
-      norm_gain.reshape(1, D), pose_weight, target_pose, foot_contact)
-    return (grad_input, gates_t[:TOP].T, loss[0, 0])
+    )(frames_in, expert_ids.T, gate_values.T, gate_weight, up_weight, down_weight,
+      norm_gain.reshape(1, D), pose_weight, target_pose, foot_contact.T)
+    return (grad_input, gates_t.T, loss[0, 0])
 
 
 def solution(mesh):

time: 252 us -> 238 us (0.944)
  Pallas kernels: 242 us -> 232 us
  local copies, waits for them, and re-layouts: 7.42 us -> 3.15 us
    pallas_call x1, Pallas kernels: 242 us -> 232 us  [per_device(): pl.pallas_call(step_kernel, out_shape=[jax.ShapeDtypeStruct((ROWS, D), BF...]
    unnamed x4 -> x2, local copies, waits for them, and re-layouts: 6.15 us -> 3.15 us
where the time goes in v3:
time: 238 us; the launch traced here: 237 us
  Pallas kernels  232 us (97%)
  local copies, waits for them, and re-layouts  3.15 us (1%)
  between operations  2.41 us (1%)
    pallas_call x1, Pallas kernels, per_device(): pl.pallas_call(step_kernel, out_shape=[jax.ShapeDtypeStruct((ROWS, D), BF...  232 us

profile of v3, /device:TPU:1, one launch (start us, length us, event | category | flops | bytes accessed | tf_op | source)
XLA Modules:
  0.0 237.3 jit_solution(13761011927436328512)
XLA Ops:
  0.6 231.8 %step.1 = (bf16[128,2048]{1,0:T(8,128)(2,1)}, f32[6,128]{1,0:T(8,128)}, f32[1,1]{1,0:T(1,128)}) custom-call(bf16[128,2048]{1,0:T(8,128)(2,1)} %rows.1, s32[6,128]{1,0:T(8,128)} %bitcast.7, f32[6,128]{1,0:T(8,128)} %bitcast.8, bf16[1,2048,768]{2,1,0:T(8,128)(2,1)} %wg_hbm.1, bf16[1,2048,768]{2,1,0:T(8,128)(2,1)} %wu_hbm.1, bf16[1,768,2048]{2,1,0:T(8,128)(2,1)} %wd_hbm.1, ...), custom_call_target="tpu_custom_call" | custom-call | tf_op jit(solution)/shard_map/step/pallas_call | solution.py:554
  232.4 1.9 copy.16
  234.3 1.3 copy.17

commit v4 on v3

--- a/solution.py
+++ b/solution.py
@@ -57,7 +57,7 @@
         index = lax.rem(self.index + offset + devices, devices)
         return {"seg": lax.div(index, RING * GROUP), "ep": lax.rem(index, RING * GROUP)}
 
-    def barrier(self):
+    def greet(self):
         semaphore = pltpu.get_barrier_semaphore()
         for o in (-1, 1):
             pl.semaphore_signal(semaphore, inc=1, device_id=self.ring(o), device_id_type=MESH)
@@ -67,7 +67,9 @@
             pl.semaphore_signal(semaphore, inc=1, device_id=self.segment(o), device_id_type=MESH)
         for o in (-1, 1):
             pl.semaphore_signal(semaphore, inc=1, device_id=self.next(o), device_id_type=MESH)
-        pl.semaphore_wait(semaphore, GROUP + self.segs + 2)
+
+    def meet(self):
+        pl.semaphore_wait(pltpu.get_barrier_semaphore(), GROUP + self.segs + 2)
 
 
 def remote(src, dst, send_sem, recv_sem, device):
@@ -167,7 +169,6 @@
     for c in range(4):
         plus(1, c).start()
         minus(1, c).start()
-    zbuf[0, 0:ROWS, :] = rows[...]
     for s in range(1, 5):
         p = s - 1
         for copy in table_copies(s):
@@ -196,34 +197,40 @@
             )
             for o in range(1, GROUP):
                 remote(gbuf.at[p, at.mate(o), :, cols(c)], xrecv.at[p, at.g, :, cols(c)],
-                       xs.at[p], xr.at[p], at.group(o)).start()
+                       xs.at[p], xr.at[p, c], at.group(o)).start()
         xrecv[p, at.g] = gbuf[p, at.g]
         if s >= 2:
-            arrive(at, p - 1, gbuf, xrecv, xs, xr)
+            for c in range(4):
+                arrive(at, p - 1, c, gbuf, xrecv, xs, xr)
             experts_of(p - 1)
-    arrive(at, 3, gbuf, xrecv, xs, xr)
-    for s in range(1, 5):
-        for copy in table_copies(s):
-            copy.wait_send()
-        for c in range(4):
-            if has_plus(s, c):
-                plus(s, c).wait_send()
-            if has_minus(s, c):
-                minus(s, c).wait_send()
-
-
-def arrive(at, p, gbuf, xrecv, xs, xr):
-    whole = remote(gbuf.at[p, pl.ds(0, GROUP - 1)], xrecv.at[p, pl.ds(0, GROUP - 1)],
-                   xs.at[p], xr.at[p], at.group(1))
-    whole.wait_send()
-    whole.wait_recv()
+
+    def drain():
+        for p in range(4):
+            remote(gbuf.at[p, pl.ds(0, GROUP - 1)], xrecv.at[p, pl.ds(0, GROUP - 1)],
+                   xs.at[p], xr.at[p, 0], at.group(1)).wait_send()
+        for s in range(1, 5):
+            for copy in table_copies(s):
+                copy.wait_send()
+            for c in range(4):
+                if has_plus(s, c):
+                    plus(s, c).wait_send()
+                if has_minus(s, c):
+                    minus(s, c).wait_send()
+
+    return drain
+
+
+def arrive(at, p, c, gbuf, xrecv, xs, xr):
+    remote(gbuf.at[p, pl.ds(0, GROUP - 1), :, cols(c)], xrecv.at[p, pl.ds(0, GROUP - 1), :, cols(c)],
+           xs.at[p], xr.at[p, c], at.group(1)).wait_recv()
 
 
 BACK_ORDER = [(3, 0), (3, 2), (3, 1), (3, 3)] + [(p, c) for p in (2, 1, 0) for c in (2, 3, 0, 1)]
 AHEAD = 6
-
-
-def combine(at, ybuf, crecv, rsend, rrecv, sems, selectors_t, between, finish):
+LAST_ORDER = (0, 2, 1, 3)
+
+
+def combine(at, ybuf, crecv, rsend, rrecv, sems, selectors_t, produce, between, finish):
     cs, cr, rs, rr = sems
     seen = set()
     waiting = list(BACK_ORDER)
@@ -231,6 +238,8 @@
     def send_back():
         if waiting:
             p, c = waiting.pop(0)
+            if p == 3:
+                produce(c)
             for o in range(1, GROUP):
                 remote(ybuf.at[p, at.mate(o), :, cols(c)], crecv.at[p, at.g, :, cols(c)],
                        cs.at[p, c], cr.at[p, c], at.group(o)).start()
@@ -240,15 +249,16 @@
     for i in range(AHEAD):
         send_back()
 
+    def whole(p, c):
+        return remote(ybuf.at[p, pl.ds(0, GROUP - 1), :, cols(c)],
+                      crecv.at[p, pl.ds(0, GROUP - 1), :, cols(c)],
+                      cs.at[p, c], cr.at[p, c], at.group(1))
+
     def partial(p, half, c):
         if (p, c) not in seen:
             seen.add((p, c))
             send_back()
-            whole = remote(ybuf.at[p, pl.ds(0, GROUP - 1), :, cols(c)],
-                           crecv.at[p, pl.ds(0, GROUP - 1), :, cols(c)],
-                           cs.at[p, c], cr.at[p, c], at.group(1))
-            whole.wait_send()
-            whole.wait_recv()
+            whole(p, c).wait_recv()
         block = crecv[p, :, :, c * CHUNK : (c + 1) * CHUNK].reshape(BLOCK, CHUNK)
         total = jnp.zeros((ROWS, CHUNK), F32)
         for selector in selectors_t:
@@ -292,20 +302,27 @@
         finish(c, total)
     for t in range(1, 5):
         for c in range(4):
+            whole(t - 1, c).wait_send()
             for way in range(2):
                 if has(way, t, c):
                     hop(way, t, c).wait_send()
 
 
-def step_kernel(rows, ids, gates, wg_hbm, wu_hbm, wd_hbm, gain, pose_weight, target, contact,
-                grad_in, gates_out, loss_out,
-                wg, wu, wd, tab, pick, pick_t, gate_hi, gate_lo, gate_hi_t, gate_lo_t,
-                zbuf, gbuf, xrecv, hidden, hidden2, gate_pre, up_pre, ybuf, crecv, crecv2, rsend, rrecv,
-                turn, state, grad_state, moe_grad, foot, foot_recv, tiles, dots, dots_recv,
+def step_kernel(rows_hbm, ids, gates, wg_hbm, wu_hbm, wd_hbm, gain, pose_hbm, target_hbm, contact,
+                grad_hbm, gates_out, loss_out,
+                wg, wu, wd, pose_weight, target, tab, pick, pick_t, gate_hi, gate_lo, gate_hi_t, gate_lo_t,
+                zbuf, gbuf, xrecv, hidden, hidden2, grad_hidden, gate_pre, up_pre, ybuf, crecv, crecv2, rsend, rrecv,
+                turn, state, grad_state, grad_in, foot, foot_recv, tiles, dots, dots_recv,
                 zs, zr, xs, xr, cs, cr, rs, rr, ts, tr, ws, fs, fr, ls, lr, ds, dr):
     at = Place()
     loads = [pltpu.make_async_copy(a.at[0], b, ws.at[i])
              for i, (a, b) in enumerate(((wg_hbm, wg), (wu_hbm, wu), (wd_hbm, wd)))]
+    loads += [pltpu.make_async_copy(pose_hbm, pose_weight, ws.at[3]),
+              pltpu.make_async_copy(target_hbm, target, ws.at[4])]
+    own = zbuf.at[0, pl.ds(0, ROWS)]
+    rows_load = pltpu.make_async_copy(rows_hbm, own, ws.at[5])
+    rows_load.start()
+    at.greet()
     for load in loads:
         load.start()
     tab_own = tab.at[0]
@@ -321,7 +338,8 @@
         here = (lanes >= 3 * k) & (lanes < 3 * k + 3)
         contacts = jnp.where(here, contact_columns[:, k : k + 1], contacts)
     turn[...] = contacts
-    at.barrier()
+    at.meet()
+    rows_load.wait()
     across = (((1,), (1,)), ((), ()))
 
     def picks(p):
@@ -355,19 +373,41 @@
 
         lax.fori_loop(0, D // 256, down_step, 0)
 
-    dispatch(at, rows, zbuf, gbuf, xrecv, (zs, zr, xs, xr), (tab, ts, tr), picks, (pick,),
-             experts_forward)
-    experts_forward(3)
+    drain = dispatch(at, own, zbuf, gbuf, xrecv, (zs, zr, xs, xr), (tab, ts, tr), picks, (pick,),
+                     experts_forward)
+    for i, c in enumerate(LAST_ORDER):
+        arrive(at, 3, c, gbuf, xrecv, xs, xr)
+
+        def up_part(n, carry):
+            window = pl.ds(pl.multiple_of(n * 256, 256), 256)
+            x = xrecv[3, :, :, c * CHUNK : (c + 1) * CHUNK].reshape(BLOCK, CHUNK)
+            a = jnp.dot(x, wg[c * CHUNK : (c + 1) * CHUNK, window], preferred_element_type=F32)
+            b = jnp.dot(x, wu[c * CHUNK : (c + 1) * CHUNK, window], preferred_element_type=F32)
+            if i > 0:
+                a = a + gate_pre[3, :, window]
+                b = b + up_pre[3, :, window]
+            gate_pre[3, :, window] = a
+            up_pre[3, :, window] = b
+            if i == 3:
+                hidden[:, window] = (a * jax.nn.sigmoid(a) * b).astype(BF16)
+            return carry
+
+        lax.fori_loop(0, FFW // 256, up_part, 0)
+
+    def last_forward(c):
+        y = jnp.dot(hidden[...], wd[:, c * CHUNK : (c + 1) * CHUNK], preferred_element_type=F32)
+        ybuf[3, :, :, c * CHUNK : (c + 1) * CHUNK] = y.astype(BF16).reshape(GROUP, PAIR, CHUNK)
+
     squares = []
 
     def finish_state(c, total):
         window = slice(c * CHUNK, (c + 1) * CHUNK)
-        sums = rows[:, window].astype(F32) + total
+        sums = zbuf[0, 0:ROWS, window].astype(F32) + total
         state[:, window] = sums
         squares.append(jnp.sum(sums * sums, axis=1, keepdims=True))
 
     combine(at, ybuf, crecv, rsend, rrecv, (cs, cr, rs, rr), (gate_hi_t, gate_lo_t),
-            lambda t: None, finish_state)
+            last_forward, lambda t: drain() if t == 1 else None, finish_state)
 
     inverse = lax.rsqrt((squares[0] + squares[1] + squares[2] + squares[3]) / D + epsilon)
     pose = jnp.zeros((ROWS, POSE), F32)
@@ -423,7 +463,7 @@
         window = slice(c * CHUNK, (c + 1) * CHUNK)
         grads = inverse * (grad_state[:, window] - state[:, window] * inverse * products)
         grad_state[:, window] = grads
-        moe_grad[:, window] = grads.astype(BF16)
+        zbuf[0, 0:ROWS, window] = grads.astype(BF16)
     to_next.wait_send()
     to_last.wait_send()
 
@@ -479,7 +519,7 @@
             return carry
 
         lax.fori_loop(0, D // 256, up_step, 0)
-        if p < 3:
+        if p < 2:
             gate_dots(p)
 
     def gate_dots(p):
@@ -496,14 +536,44 @@
         if p == 0:
             shares.append(share(0, at.z, RING, at.ring, tile))
 
-    dispatch(at, moe_grad, zbuf, gbuf, xrecv, (zs, zr, xs, xr), None, share_loss, (gate_hi, gate_lo),
-             experts_backward)
-    experts_backward(3)
+    drain = dispatch(at, own, zbuf, gbuf, xrecv, (zs, zr, xs, xr), None, share_loss,
+                     (gate_hi, gate_lo), experts_backward)
+    for i, c in enumerate(LAST_ORDER):
+        arrive(at, 3, c, gbuf, xrecv, xs, xr)
+
+        def down_part(n, carry):
+            window = pl.ds(pl.multiple_of(n * 256, 256), 256)
+            x = xrecv[3, :, :, c * CHUNK : (c + 1) * CHUNK].reshape(BLOCK, CHUNK)
+            grad = lax.dot_general(x, wd[window, c * CHUNK : (c + 1) * CHUNK], across,
+                                   preferred_element_type=F32)
+            if i > 0:
+                grad = grad + grad_hidden[:, window]
+            if i < 3:
+                grad_hidden[:, window] = grad
+            else:
+                a = gate_pre[3, :, window]
+                s = jax.nn.sigmoid(a)
+                hidden[:, window] = (grad * up_pre[3, :, window] * (s * (1.0 + a * (1.0 - s)))).astype(BF16)
+                hidden2[:, window] = (grad * (a * s)).astype(BF16)
+            return carry
+
+        lax.fori_loop(0, FFW // 256, down_part, 0)
+
+    def last_backward(c):
+        y = lax.dot_general(hidden[...], wg[c * CHUNK : (c + 1) * CHUNK, :], across,
+                            preferred_element_type=F32)
+        y = y + lax.dot_general(hidden2[...], wu[c * CHUNK : (c + 1) * CHUNK, :], across,
+                                preferred_element_type=F32)
+        ybuf[3, :, :, c * CHUNK : (c + 1) * CHUNK] = y.astype(BF16).reshape(GROUP, PAIR, CHUNK)
+
     dot_sends = [remote(dots.at[PLACE[o]], dots_recv.at[PLACE[RING - o]], ds.at[o],
                         dr.at[PLACE[RING - o]], at.ring(o)) for o in range(1, RING)]
 
     def last_dots(t):
+        if t == 2:
+            drain()
         if t == 1:
+            gate_dots(2)
             gate_dots(3)
             for send in dot_sends:
                 send.start()
@@ -511,8 +581,13 @@
     def finish_input(c, total):
         window = slice(c * CHUNK, (c + 1) * CHUNK)
         grad_in[:, window] = (grad_state[:, window] + total).astype(BF16)
-
-    combine(at, ybuf, crecv2, rsend, rrecv, (cs, cr, rs, rr), (pick_t,), last_dots, finish_input)
+        store(c).start()
+
+    def store(c):
+        return pltpu.make_async_copy(grad_in.at[:, cols(c)], grad_hbm.at[:, cols(c)], ws.at[c])
+
+    combine(at, ybuf, crecv2, rsend, rrecv, (cs, cr, rs, rr), (pick_t,), last_backward,
+            last_dots, finish_input)
     loss = gather_tile(2, at.segs, shares.pop())
     loss_out[0, 0] = jnp.sum(loss) * (0.5 / (frames_all * POSE))
     for send in dot_sends:
@@ -521,6 +596,8 @@
     for o in range(1, RING):
         total = total + dots_recv[PLACE[RING - o]]
     gates_out[...] = total[0:TOP]
+    for c in range(4):
+        store(c).wait()
     for send in dot_sends:
         send.wait_send()
 
@@ -558,19 +635,20 @@
             jax.ShapeDtypeStruct((TOP, ROWS), F32),
             jax.ShapeDtypeStruct((1, 1), F32),
         ],
-        in_specs=[VMEM, VMEM, VMEM, ANY, ANY, ANY, VMEM, VMEM, VMEM, VMEM],
-        out_specs=[VMEM, VMEM, SMEM],
+        in_specs=[ANY, VMEM, VMEM, ANY, ANY, ANY, VMEM, ANY, ANY, VMEM],
+        out_specs=[ANY, VMEM, SMEM],
         scratch_shapes=[
             pltpu.VMEM((D, FFW), BF16), pltpu.VMEM((D, FFW), BF16), pltpu.VMEM((FFW, D), BF16),
+            pltpu.VMEM((D, POSE), BF16), pltpu.VMEM((ROWS, POSE), F32),
             pltpu.VMEM((RING, 16, ROWS), F32),
             selector, selector, selector, selector, selector, selector,
-            pltpu.VMEM((4, 2 * ROWS, D), BF16), pairs, pairs, hidden, hidden, pres, pres,
+            pltpu.VMEM((4, 2 * ROWS, D), BF16), pairs, pairs, hidden, hidden, pltpu.VMEM((BLOCK, FFW), F32), pres, pres,
             pairs, pairs, pairs, hops, hops,
             pltpu.VMEM((ROWS, ROWS), F32), wide, wide, pltpu.VMEM((ROWS, D), BF16),
             pltpu.VMEM((24, ROWS), F32), pltpu.VMEM((24, ROWS), F32),
             pltpu.VMEM((3, 8, 8, ROWS), F32), dots, dots,
-            DMA((2, 4, 4)), DMA((2, 4, 4)), DMA((4,)), DMA((4,)), DMA((4, 4)), DMA((4, 4)),
-            DMA((2, 4, 4)), DMA((2, 4, 4)), DMA((2, 4)), DMA((2, 4)), DMA((3,)),
+            DMA((2, 4, 4)), DMA((2, 4, 4)), DMA((4,)), DMA((4, 4)), DMA((4, 4)), DMA((4, 4)),
+            DMA((2, 4, 4)), DMA((2, 4, 4)), DMA((2, 4)), DMA((2, 4)), DMA((6,)),
             DMA((2,)), DMA((2,)), DMA((3, 8)), DMA((3,)), DMA((RING,)), DMA((RING,)),
         ],
         compiler_params=pltpu.CompilerParams(

time: 238 us -> 231 us (0.971)
  Pallas kernels: 232 us -> 225 us
    pallas_call x1, Pallas kernels: 232 us -> 225 us  [per_device(): pl.pallas_call(step_kernel, out_shape=[jax.ShapeDtypeStruct((ROWS, D), BF...]
where the time goes in v4:
time: 231 us; the launch traced here: 230 us
  Pallas kernels  225 us (97%)
  local copies, waits for them, and re-layouts  3.15 us (1%)
  between operations  2.41 us (1%)
    pallas_call x1, Pallas kernels, per_device(): pl.pallas_call(step_kernel, out_shape=[jax.ShapeDtypeStruct((ROWS, D), BF...  225 us

profile of v4, /device:TPU:1, one launch (start us, length us, event | category | flops | bytes accessed | tf_op | source)
XLA Modules:
  0.0 230.4 jit_solution(8895191379975114649)
XLA Ops:
  0.6 224.8 %step.1 = (bf16[128,2048]{1,0:T(8,128)(2,1)}, f32[6,128]{1,0:T(8,128)}, f32[1,1]{1,0:T(1,128)}) custom-call(bf16[128,2048]{1,0:T(8,128)(2,1)} %rows_hbm.1, s32[6,128]{1,0:T(8,128)} %bitcast.7, f32[6,128]{1,0:T(8,128)} %bitcast.8, bf16[1,2048,768]{2,1,0:T(8,128)(2,1)} %wg_hbm.1, bf16[1,2048,768]{2,1,0:T(8,128)(2,1)} %wu_hbm.1, bf16[1,768,2048]{2,1,0:T(8,128)(2,1)} %wd_hbm.1, ...), custom_call_target="tpu_custom_call" | custom-call | tf_op jit(solution)/shard_map/step/pallas_call | solution.py:631
  225.5 1.9 copy.16
  227.4 1.3 copy.17
